TPU v7x, 256 devices: a whole 4x4x8 slice. The times are simulated.
256 devices in a mesh: pb: 8 (over x, y_lo), ka: 4 (over y_hi, core), ha: 8 (over z).
Axes of the slice: x: 4, y: 4 (y_hi: 2, y_lo: 2; y = y_hi * 2 + y_lo), z: 8, core: 2. Of those that a mesh axis runs over, the one named last changes fastest.
Arguments:
- queries: bfloat16 [4096, 64, 128], P(('pb', 'ka'), 'ha'), may hold values from -8 to 8
- keys: bfloat16 [4096, 8, 128], P(('pb', 'ka'), 'ha'), may hold values from -4.5 to 4.5
- values: bfloat16 [4096, 8, 128], P(('pb', 'ka'), 'ha'), may hold values from -12 to 12
- out_grad: bfloat16 [4096, 64, 128], P(('pb', 'ka'), 'ha'), may hold values from -6 to 6
Outputs:
- attended: bfloat16 [4096, 64, 128], P(('pb', 'ka'), 'ha')
- query_grad: bfloat16 [4096, 64, 128], P(('pb', 'ka'), 'ha')
- key_grad: bfloat16 [4096, 8, 128], P(('pb', 'ka'), 'ha')
- value_grad: bfloat16 [4096, 8, 128], P(('pb', 'ka'), 'ha')
All inputs are finite; a program needn't handle non-finite values.
Results may differ from a plain program's by a relative error of at most 0.0097.
Values may be sent and summed in bfloat16 or wider, within the bound.
No kernel may reach another device: no remote copies, remote signals or barrier semaphores. Data moves between devices by JAX's collectives and lax.ppermute only.
A program may use at most 128 MiB of HBM per device.

v0:
```python
import math

import jax
import jax.numpy as jnp
from jax import lax
from jax.sharding import PartitionSpec as P

HEAD_DIM = 128
GROUP = 8


def merged(value, axis, join):
    pieces = jax.tree.map(lambda part: lax.all_gather(part, axis), value)
    head = jax.tree.map(lambda part: part[0], pieces)
    tail = jax.tree.map(lambda part: part[1:], pieces)
    total, _ = lax.scan(lambda total, section: (join(total, section), None), head, tail)
    return total


def combine_partials(earlier, second):
    earlier_max, earlier_total, earlier_sum = earlier
    second_max, second_total, second_sum = second
    joined = jnp.maximum(earlier_max, second_max)
    earlier_factor = jnp.exp(earlier_max - joined)
    second_factor = jnp.exp(second_max - joined)
    merged_total = earlier_total * earlier_factor + second_total * second_factor
    merged_sum = earlier_sum * earlier_factor[..., None] + second_sum * second_factor[..., None]
    return (joined, merged_total, merged_sum)


def make_absorb(grouped, scaling, running, pieces):
    run_max, run_total, run_sum = running
    key_piece, value_piece = pieces
    scores = (
        jnp.einsum("qhgd,khd->hgqk", grouped, key_piece, preferred_element_type=jnp.float32)
        * scaling
    )
    new_max = jnp.max(scores, axis=-1)
    factor = jnp.exp(run_max - new_max)
    weights = jnp.exp(scores - new_max[..., None])
    run_total = run_total * factor + jnp.sum(weights, axis=-1)
    run_sum = run_sum * factor[..., None] + jnp.einsum(
        "hgqk,khd->hgqd",
        weights,
        value_piece.astype(jnp.float32),
        preferred_element_type=jnp.float32,
        precision=lax.Precision.HIGHEST,
    )
    return (new_max, run_total, run_sum)


def start_stats(kv_count, query_total):
    stat_shape = (kv_count, GROUP, query_total)
    return (
        jnp.full(stat_shape, -jnp.inf, jnp.float32),
        jnp.zeros(stat_shape, jnp.float32),
        jnp.zeros(stat_shape + (HEAD_DIM,), jnp.float32),
    )


def backward_blocks(query_heads, grad_heads, log_total, row_dots, key_rows, value_rows, scaling):
    key_total = key_rows.shape[0]
    block_width = math.gcd(key_total, 512)

    def visit_block(grad_running, position):
        first_row = position * block_width
        key_block = lax.dynamic_slice_in_dim(key_rows, first_row, block_width, 0)
        value_block = lax.dynamic_slice_in_dim(value_rows, first_row, block_width, 0)
        scores = (
            jnp.einsum("qhgd,khd->hgqk", query_heads, key_block, preferred_element_type=jnp.float32)
            * scaling
        )
        probs = jnp.exp(scores - log_total[..., None])
        value_part = jnp.einsum(
            "hgqk,qhgd->khd",
            probs.astype(jnp.bfloat16),
            grad_heads,
            preferred_element_type=jnp.float32,
        )
        grad_probs = jnp.einsum(
            "qhgd,khd->hgqk", grad_heads, value_block, preferred_element_type=jnp.float32
        )
        grad_scores = (scaling * probs * (grad_probs - row_dots[..., None])).astype(jnp.bfloat16)
        grad_running = grad_running + jnp.einsum(
            "hgqk,khd->qhgd", grad_scores, key_block, preferred_element_type=jnp.float32
        )
        key_part = jnp.einsum(
            "hgqk,qhgd->khd", grad_scores, query_heads, preferred_element_type=jnp.float32
        )
        return (grad_running, (key_part, value_part))

    initial = jnp.zeros(query_heads.shape, jnp.float32)
    block_count = key_total // block_width
    grad_query, (key_parts, value_parts) = lax.scan(
        visit_block, initial, jnp.arange(block_count, dtype=jnp.int32)
    )
    tail_shape = key_rows.shape
    return (grad_query, key_parts.reshape(tail_shape), value_parts.reshape(tail_shape))


def on_device(queries, keys, values, out_grad):
    local_rows = queries.shape[0]
    head_count = queries.shape[1]
    kv_count = keys.shape[1]
    scaling = HEAD_DIM ** (-0.5)
    own_queries = queries.reshape(local_rows, kv_count, GROUP, HEAD_DIM)
    block_queries = lax.all_gather(queries, "ka", axis=0, tiled=True)
    query_total = block_queries.shape[0]
    grouped = block_queries.reshape(query_total, kv_count, GROUP, HEAD_DIM)
    local_parts = make_absorb(
        grouped,
        scaling,
        start_stats(kv_count, query_total),
        (
            lax.all_gather(keys, "pb", axis=0, tiled=True),
            lax.all_gather(values, "pb", axis=0, tiled=True),
        ),
    )
    whole_max, whole_total, whole_sum = merged(local_parts, "ka", combine_partials)
    first_row = lax.axis_index("ka") * local_rows
    own_max = lax.dynamic_slice_in_dim(whole_max, first_row, local_rows, 2)
    own_total = lax.dynamic_slice_in_dim(whole_total, first_row, local_rows, 2)
    own_sum = lax.dynamic_slice_in_dim(whole_sum, first_row, local_rows, 2)
    exact_out = own_sum / own_total[..., None]
    output_heads = exact_out.astype(jnp.bfloat16)
    log_total = own_max + jnp.log(own_total)
    attended = jnp.transpose(output_heads, (2, 0, 1, 3)).reshape(local_rows, head_count, HEAD_DIM)
    grad_heads = out_grad.reshape(local_rows, kv_count, GROUP, HEAD_DIM)
    row_dots = jnp.einsum(
        "hgqd,qhgd->hgq",
        exact_out,
        grad_heads.astype(jnp.float32),
        preferred_element_type=jnp.float32,
    )
    wide_key, wide_value = (
        lax.all_gather(keys, ("pb", "ka"), axis=0, tiled=True),
        lax.all_gather(values, ("pb", "ka"), axis=0, tiled=True),
    )
    grad_query, key_terms, value_terms = backward_blocks(
        own_queries, grad_heads, log_total, row_dots, wide_key, wide_value, scaling
    )
    grad_key, grad_value = (
        lax.psum_scatter(key_terms, ("pb", "ka"), scatter_dimension=0, tiled=True),
        lax.psum_scatter(value_terms, ("pb", "ka"), scatter_dimension=0, tiled=True),
    )
    query_grad = grad_query.astype(jnp.bfloat16).reshape(local_rows, head_count, HEAD_DIM)
    return (attended, query_grad, grad_key.astype(jnp.bfloat16), grad_value.astype(jnp.bfloat16))


def solution(mesh):
    return jax.shard_map(
        on_device,
        mesh=mesh,
        in_specs=(
            P(("pb", "ka"), "ha", None),
            P(("pb", "ka"), "ha", None),
            P(("pb", "ka"), "ha", None),
            P(("pb", "ka"), "ha", None),
        ),
        out_specs=(
            P(("pb", "ka"), "ha", None),
            P(("pb", "ka"), "ha", None),
            P(("pb", "ka"), "ha", None),
            P(("pb", "ka"), "ha", None),
        ),
        check_vma=False,
    )
```

profile of v0, /device:TPU:32, one launch (start us, length us, event | category | flops | bytes accessed | tf_op | source)
XLA Modules:
  0.0 639.3 jit_solution(16966723260642444875)
XLA Ops:
  7.2 1.7 copy.52
  9.0 28.9 %all_gather.31 = bf16[1024,1,128]{2,0,1:T(8,128)(2,1)S(1)} all-gather(bf16[128,1,128]{2,0,1:T(8,128)(2,1)} %param.9), channel_id=1, replica_groups=mesh['pb'=8,'ka'=4,'ha'=8] {'pb'}, dimensions={0}, use_global_device_ids=true | all-gather | bytes 294912 | tf_op jit(solution)/shard_map/all_gather | solution.py:115
  37.9 28.7 %all_gather.36 = bf16[1024,1,128]{2,0,1:T(8,128)(2,1)S(1)} all-gather(bf16[128,1,128]{2,0,1:T(8,128)(2,1)} %param.10), channel_id=1, replica_groups=mesh['pb'=8,'ka'=4,'ha'=8] {'pb'}, dimensions={0}, use_global_device_ids=true | all-gather | bytes 294912 | tf_op jit(solution)/shard_map/all_gather | solution.py:116
  66.6 9.3 %bitcast_reduce_fusion = (f32[8,512]{1,0:T(8,128)S(1)}, f32[1024,512,8]{1,0,2:T(8,128)}) fusion(bf16[512,8,128]{2,0,1:T(8,128)(2,1)} %all-gather.7.cloned.1.call-done, bf16[1024,1,128]{2,0,1:T(8,128)(2,1)S(1)} %all_gather.31), kind=kOutput, calls=%fused_computation.44 | convolution fusion | flops 1082126336 | bytes 18104320 | tf_op jit(solution)/shard_map/qhgd,khd->hgqk/dot_general | solution.py:35
  75.9 8.5 %fusion.36 = f32[8,512]{1,0:T(8,128)S(1)} fusion(f32[1024,512,8]{1,0,2:T(8,128)} %get-tuple-element.212, f32[8,512]{1,0:T(8,128)S(1)} %get-tuple-element.211), kind=kLoop, calls=%fused_computation.46 | loop fusion | flops 12578816 | bytes 16809984 | tf_op jit(solution)/shard_map/reduce_sum | solution.py:41
  84.4 18.9 %fusion.39 = f32[8,512,128]{2,1,0:T(8,128)} fusion(f32[1024,512,8]{1,0,2:T(8,128)} %get-tuple-element.212, f32[8,512]{1,0:T(8,128)S(1)} %get-tuple-element.211, f32[8,512]{1,0:T(8,128)S(1)} %get-tuple-element.209, bf16[1024,1,128]{2,0,1:T(8,128)(2,1)S(1)} %all_gather.36), kind=kOutput, calls=%fused_computation.50 | convolution fusion | flops 6451363840 | bytes 19169280 | tf_op jit(solution)/shard_map/hgqk,khd->hgqd/dot_general | solution.py:42
  104.8 6.7 %all_gather.35 = f32[4,1,8,512]{3,2,1,0:T(8,128)S(1)} all-gather(f32[1,1,8,512]{3,2,1,0:T(8,128)S(1)} %get-tuple-element.210), channel_id=1, replica_groups=mesh['pb'=8,'ka'=4,'ha'=8] {'ka'}, dimensions={0}, use_global_device_ids=true | all-gather | bytes 81920 | tf_op jit(solution)/shard_map/all_gather | solution.py:13
  111.5 6.8 %all-gather = f32[32,512]{1,0:T(8,128)S(1)} all-gather(f32[8,512]{1,0:T(8,128)S(1)} %get-tuple-element.211), channel_id=2, replica_groups=mesh['pb'=8,'ka'=4,'ha'=8] {'ka'}, dimensions={0}, use_global_device_ids=true | all-gather | bytes 81920 | tf_op jit(solution)/shard_map/all_gather | solution.py:13
  118.3 52.3 %all-gather.13.cloned.1.call-done = f32[32,512,128]{2,1,0:T(8,128)} async-done(((f32[8,512,128]{2,1,0:T(8,128)}), f32[32,512,128]{2,1,0:T(8,128)}) %all-gather.13.cloned.1.call-update) | async-done | bytes 8388624 | tf_op jit(solution)/shard_map/all_gather | solution.py:13
  170.6 6.1 slice.33
  176.7 1.7 slice_bitcast_fusion
  178.4 8.6 %while.29 = (s32[]{:T(128)}, f32[1,8,512]{2,1,0:T(8,128)S(1)}, f32[1,8,512]{2,1,0:T(8,128)S(1)}, f32[1,8,512,128]{3,2,1,0:T(8,128)S(1)}, f32[3,1,8,512]{3,2,1,0:...) while((s32[]{:T(128)}, f32[1,8,512]{2,1,0:T(8,128)S(1)}, ...), condition=%wide.region_3.4_spmd, body=%wide.region_2.3_spmd.sunk | while | flops 1601538 | bytes 6537313 | solution.py:16
  178.7 2.7 fusion.70
  181.5 2.7 fusion.70
  184.3 2.7 fusion.70
  187.0 2.5 copy.33
  189.7 1.4 fusion.42
  191.2 38.9 %all-gather.11.cloned.1.call-done = bf16[4096,1,128]{2,0,1:T(8,128)(2,1)} async-done(((bf16[128,1,128]{2,0,1:T(8,128)(2,1)}), bf16[4096,1,128]{2,0,1:T(8,128)(2,1)}) %all-gather.11.cloned.1.call-update) | async-done | bytes 1048592 | tf_op jit(solution)/shard_map/all_gather | solution.py:137
  230.1 59.3 %all-gather.9.cloned.1.call-done = bf16[4096,1,128]{2,0,1:T(8,128)(2,1)} async-done(((bf16[128,1,128]{2,0,1:T(8,128)(2,1)}), bf16[4096,1,128]{2,0,1:T(8,128)(2,1)}) %all-gather.9.cloned.1.call-update) | async-done | bytes 1048592 | tf_op jit(solution)/shard_map/all_gather | solution.py:136
  289.5 63.0 %while.30 = (s32[]{:T(128)}, f32[128,1,8,128]{0,3,2,1:T(8,128)S(1)}, f32[8,512,1,128]{3,1,2,0:T(8,128)}, f32[8,512,1,128]{3,1,2,0:T(8,128)}, s32[8]{0:T(128)S(1)...) while((s32[]{:T(128)}, ...), condition=%wide.region_5.6_spmd.clone, body=%wide.region_4.5_spmd.clone.sunk | while | flops 676069376 | bytes 12465373 | solution.py:94
  290.7 1.3 fusion.81
  292.0 1.6 fusion.82
  293.7 1.2 fusion.84
  294.8 1.2 fusion.85
  296.0 1.3 fusion.83
  298.6 1.3 fusion.81
  299.9 1.6 fusion.82
  302.7 1.2 fusion.85
  303.9 1.3 fusion.83
  306.4 1.3 fusion.81
  307.8 1.6 fusion.82
  309.4 1.2 fusion.84
  310.6 1.2 fusion.85
  311.7 1.3 fusion.83
  314.3 1.3 fusion.81
  315.7 1.6 fusion.82
  317.3 1.2 fusion.84
  318.4 1.2 fusion.85
  319.6 1.3 fusion.83
  322.2 1.3 fusion.81
  323.5 1.6 fusion.82
  325.2 1.2 fusion.84
  326.3 1.2 fusion.85
  327.5 1.3 fusion.83
  330.1 1.3 fusion.81
  331.4 1.6 fusion.82
  333.0 1.2 fusion.84
  334.2 1.2 fusion.85
  335.4 1.3 fusion.83
  338.0 1.3 fusion.81
  339.3 1.6 fusion.82
  340.9 1.2 fusion.84
  342.1 1.2 fusion.85
  343.3 1.3 fusion.83
  345.9 1.3 fusion.81
  347.2 1.6 fusion.82
  348.8 1.2 fusion.84
  350.0 1.2 fusion.85
  351.2 1.3 fusion.83
  354.0 2.0 convert_bitcast_fusion.1
  356.0 136.3 %reduce-scatter.3.cloned.1.call-done = f32[128,1,128]{2,0,1:T(8,128)} async-done(((f32[4096,1,128]{2,0,1:T(8,128)}), f32[128,1,128]{2,0,1:T(8,128)}) %reduce-scatter.3.cloned.1.call-update) | async-done | bytes 65552 | tf_op jit(solution)/shard_map/reduce_scatter | solution.py:143
  492.3 1.5 convert_element_type.22
  493.7 137.3 %reduce-scatter.5.cloned.1.call-done = f32[128,1,128]{2,0,1:T(8,128)} async-done(((f32[4096,1,128]{2,0,1:T(8,128)}), f32[128,1,128]{2,0,1:T(8,128)}) %reduce-scatter.5.cloned.1.call-update) | async-done | bytes 65552 | tf_op jit(solution)/shard_map/reduce_scatter | solution.py:144
  631.0 1.5 convert_element_type.23
  (49 shorter events, 9.1 us)
Async XLA Ops:
  7.2 59.4 %all-gather.7.cloned.1.call-start = ((), (), s32[]{:S(2)}) async-start(), calls=%async_computation.2 | async-start | bytes 1310720 | tf_op jit(solution)/shard_map/all_gather | solution.py:107
  8.9 161.7 %all-gather.13.cloned.1.call-start = ((), (), s32[]{:S(2)}) async-start(), calls=%async_computation.7 | async-start | bytes 10485760 | tf_op jit(solution)/shard_map/all_gather | solution.py:13
  103.3 1.4 copy-start.1
  103.3 126.8 %all-gather.11.cloned.1.call-start = ((), (), s32[]{:S(2)}) async-start(), calls=%async_computation.4 | async-start | bytes 1081344 | tf_op jit(solution)/shard_map/all_gather | solution.py:137
  104.1 185.4 %all-gather.9.cloned.1.call-start = ((), (), s32[]{:S(2)}) async-start(), calls=%async_computation.3 | async-start | bytes 1081344 | tf_op jit(solution)/shard_map/all_gather | solution.py:136
  104.7 387.6 %reduce-scatter.3.cloned.1.call-start = ((), (), s32[]{:S(2)}) async-start(), calls=%async_computation.5 | async-start | bytes 2162688 | tf_op jit(solution)/shard_map/reduce_scatter | solution.py:143
  187.0 102.4 %copy-start = (bf16[128,8,128]{2,0,1:T(8,128)(2,1)S(1)}, bf16[128,8,128]{2,0,1:T(8,128)(2,1)}, u32[]{:S(2)}) copy-start(bf16[128,8,128]{2,0,1:T(8,128)(2,1)} %copy.52) | copy-start | bytes 786436
  352.5 278.5 %reduce-scatter.5.cloned.1.call-start = ((), (), s32[]{:S(2)}) async-start(), calls=%async_computation.6 | async-start | bytes 2162688 | tf_op jit(solution)/shard_map/reduce_scatter | solution.py:144
Sparse Core Ops, SparseCore 0:
  10.4 27.1 all-gather.6
  103.5 67.0 all-gather.12
  172.5 57.5 all-gather.10
  231.8 57.5 all-gather.8
  352.6 139.5 reduce-scatter.2
  494.6 136.3 reduce-scatter.4
where the time goes:
time: 640 us; the launch traced here: 639 us
  waiting for transfers between devices  426 us (67%)
  matrix products  81 us (13%)
  blocking collectives  71.1 us (11%)
  other arithmetic  23 us (4%)
  local copies, waits for them, and re-layouts  17.9 us (3%)
  between operations  14.2 us (2%)
    reduce_scatter x1, waiting for transfers between devices, on_device(): lax.psum_scatter(value_terms, ('pb', 'ka'), scatter_dimension=0, tiled=True)  137 us
    reduce_scatter x1, waiting for transfers between devices, on_device(): lax.psum_scatter(key_terms, ('pb', 'ka'), scatter_dimension=0, tiled=True)  136 us
    all_gather x1, waiting for transfers between devices, on_device(): lax.all_gather(keys, ('pb', 'ka'), axis=0, tiled=True)  59.3 us
    all_gather x1, waiting for transfers between devices, merged(): pieces = jax.tree.map(lambda part: lax.all_gather(part, axis), value)  52.3 us
    all_gather x1, waiting for transfers between devices, on_device(): lax.all_gather(values, ('pb', 'ka'), axis=0, tiled=True)  38.9 us
    all_gather x1, blocking collectives, on_device(): lax.all_gather(keys, 'pb', axis=0, tiled=True)  28.9 us
    all_gather x1, blocking collectives, on_device(): lax.all_gather(values, 'pb', axis=0, tiled=True)  28.7 us
    dot_general x1, matrix products, make_absorb(): jnp.einsum('hgqk,khd->hgqd', weights, value_piece.astype(jnp.float32), pr...  18.9 us
  transfers between devices with their start and end apart: 6, of which 5 were waited for; matrix products, arithmetic and copies ran while one was open for 4% of the time, Pallas kernels for 0%

commit v1 on v0

v1 whole, which is shorter than its diff:
```python
import math

import jax
import jax.numpy as jnp
from jax import lax
from jax.experimental import pallas as pl
from jax.experimental.pallas import tpu as pltpu
from jax.sharding import Mesh, PartitionSpec as P

HEAD_DIM = 128
SCALE = HEAD_DIM ** (-0.5)
EXP2_SCALE = SCALE * math.log2(math.e)
CHIPS = ("x", "yl", "yh")
NCHIP = 16
ROWS = 128
QB = 256
KB = 512
F32 = jnp.float32
BF16 = jnp.bfloat16


def dot(a, b):
    return jnp.dot(a, b, preferred_element_type=F32)


def dot_t(a, b):
    return lax.dot_general(a, b, (((1,), (1,)), ((), ())), preferred_element_type=F32)


def attention_kernel(
    q_ref, g_ref, kva_ref, kvb_ref,
    out_ref, dq_ref, da_ref, db_ref,
    kt, vt, s_buf, p_buf, ds_buf, gn_buf, d_buf, dqt,
):
    rows = q_ref.shape[0]
    nq = rows // QB
    per = KB // ROWS
    half_chunks = NCHIP // per

    vt[HEAD_DIM:, :] = jnp.ones((vt.shape[0] - HEAD_DIM, vt.shape[1]), BF16)
    for half, ref in enumerate((kva_ref, kvb_ref)):
        @pl.loop(0, NCHIP)
        def _(b, half=half, ref=ref):
            col = pl.multiple_of((half * NCHIP + b) * ROWS, ROWS)
            kt[:, pl.ds(col, ROWS)] = jnp.transpose(ref[b, :ROWS, :])
            vt[:HEAD_DIM, pl.ds(col, ROWS)] = jnp.transpose(ref[b, ROWS:, :])

    def keys(ref, c):
        return ref[pl.ds(c * per, per), :ROWS, :].reshape(KB, HEAD_DIM)

    def vals(ref, c):
        return ref[pl.ds(c * per, per), ROWS:, :].reshape(KB, HEAD_DIM)

    for b in range(nq):
        qs = slice(b * QB, (b + 1) * QB)
        qb = q_ref[qs, :]

        top = jnp.full((8, QB), -jnp.inf, F32)
        for half, ref in enumerate((kva_ref, kvb_ref)):
            def scores(c, top, half=half, ref=ref):
                row = pl.multiple_of((half * half_chunks + c) * KB, KB)
                s = dot_t(keys(ref, c), qb)
                s_buf[pl.ds(row, KB), :] = s
                return jnp.maximum(top, jnp.max(s.reshape(KB // 8, 8, QB), axis=0))
            top = lax.fori_loop(0, half_chunks, scores, top)
        peak = jnp.max(top, axis=0, keepdims=True) * EXP2_SCALE

        def weigh(c, acc):
            row = pl.multiple_of(c * KB, KB)
            p = jnp.exp2(s_buf[pl.ds(row, KB), :] * EXP2_SCALE - peak).astype(BF16)
            p_buf[pl.ds(row, KB), qs] = p
            return acc + dot(vt[:, pl.ds(row, KB)], p)
        acc = lax.fori_loop(0, 2 * half_chunks, weigh, jnp.zeros((vt.shape[0], QB), F32))

        inv = 1.0 / acc[HEAD_DIM:HEAD_DIM + 1, :]
        out_t = acc[:HEAD_DIM, :] * inv
        out_ref[qs, :] = jnp.transpose(out_t).astype(BF16)
        inv_rows = jnp.transpose(jnp.broadcast_to(inv, (HEAD_DIM, QB)))
        gn = (g_ref[qs, :].astype(F32) * inv_rows).astype(BF16)
        gn_buf[qs, :] = gn
        gn_t = jnp.transpose(gn.astype(F32))
        d_buf[:, qs] = jnp.broadcast_to(jnp.sum(gn_t * out_t, axis=0, keepdims=True), (8, QB))

    dqt[...] = jnp.zeros_like(dqt)
    for half, (ref, dref) in enumerate(((kva_ref, da_ref), (kvb_ref, db_ref))):
        def back(c, carry, half=half, ref=ref, dref=dref):
            row = pl.multiple_of((half * half_chunks + c) * KB, KB)
            v = vals(ref, c)
            dv = dot(p_buf[pl.ds(row, KB), :], gn_buf[...])
            dref[pl.ds(c * per, per), ROWS:, :] = dv.astype(BF16).reshape(per, ROWS, HEAD_DIM)
            for b in range(nq):
                qs = slice(b * QB, (b + 1) * QB)
                dp = dot_t(v, gn_buf[qs, :])
                ds = (p_buf[pl.ds(row, KB), qs].astype(F32) * (dp - d_buf[0:1, qs])).astype(BF16)
                ds_buf[:, qs] = ds
                dqt[:, qs] += dot(kt[:, pl.ds(row, KB)], ds)
            dk = dot(ds_buf[...], q_ref[...]) * SCALE
            dref[pl.ds(c * per, per), :ROWS, :] = dk.astype(BF16).reshape(per, ROWS, HEAD_DIM)
            return carry
        lax.fori_loop(0, half_chunks, back, 0)
    for b in range(nq):
        qs = slice(b * QB, (b + 1) * QB)
        dq_ref[qs, :] = (jnp.transpose(dqt[:, qs]) * SCALE).astype(BF16)


def attention(q, g, kva, kvb):
    rows = q.shape[0]
    total = 2 * NCHIP * ROWS
    vmem = pl.BlockSpec(memory_space=pltpu.VMEM)
    return pl.pallas_call(
        attention_kernel,
        out_shape=(
            jax.ShapeDtypeStruct(q.shape, BF16),
            jax.ShapeDtypeStruct(q.shape, BF16),
            jax.ShapeDtypeStruct(kva.shape, BF16),
            jax.ShapeDtypeStruct(kvb.shape, BF16),
        ),
        in_specs=[vmem] * 4,
        out_specs=(vmem,) * 4,
        scratch_shapes=[
            pltpu.VMEM((HEAD_DIM, total), BF16),
            pltpu.VMEM((HEAD_DIM + 16, total), BF16),
            pltpu.VMEM((total, QB), F32),
            pltpu.VMEM((total, rows), BF16),
            pltpu.VMEM((KB, rows), BF16),
            pltpu.VMEM((rows, HEAD_DIM), BF16),
            pltpu.VMEM((8, rows), F32),
            pltpu.VMEM((HEAD_DIM, rows), F32),
        ],
        cost_estimate=pl.CostEstimate(
            flops=12 * rows * total * HEAD_DIM, transcendentals=rows * total, bytes_accessed=6 << 20
        ),
        compiler_params=pltpu.CompilerParams(vmem_limit_bytes=56 << 20),
    )(q, g, kva, kvb)


def swap_cores(a):
    return lax.ppermute(a, "c", [(0, 1), (1, 0)])


def exchange(a):
    return lax.all_to_all(a, CHIPS, 0, 0, tiled=True)


def on_device(queries, keys, values, out_grad):
    kv = jnp.concatenate([keys[:, 0, :], values[:, 0, :]], axis=0)
    kva = exchange(jnp.broadcast_to(kv[None], (NCHIP,) + kv.shape))
    kvb = swap_cores(kva)
    q = queries.reshape(-1, HEAD_DIM)
    g = out_grad.reshape(-1, HEAD_DIM)
    out, dq, da, db = attention(q, g, kva, kvb)
    mine = swap_cores(db)
    terms = exchange((da.astype(F32) + mine.astype(F32)).astype(BF16))
    total = jnp.sum(terms.astype(F32), axis=0).astype(BF16)
    return (
        out.reshape(queries.shape),
        dq.reshape(queries.shape),
        total[:ROWS].reshape(keys.shape),
        total[ROWS:].reshape(values.shape),
    )


def solution(mesh):
    fine = Mesh(mesh.devices.reshape(4, 2, 2, 2, 8), CHIPS + ("c", "z"))
    spec = P(CHIPS + ("c",), "z", None)
    return jax.shard_map(
        on_device,
        mesh=fine,
        in_specs=(spec,) * 4,
        out_specs=(spec,) * 4,
        check_vma=False,
    )
```

time: 640 us -> 93.8 us (0.15)
  waiting for transfers between devices: 426 us -> 5.38 us
  matrix products: 81 us -> 0 us
  Pallas kernels: 0 us -> 38.3 us
  blocking collectives: 71.1 us -> 44.8 us
  other arithmetic: 23 us -> 2.43 us
  local copies, waits for them, and re-layouts: 17.9 us -> 1.84 us
  between operations: 14.2 us -> 0.65 us
    reduce_scatter x2 -> x0, waiting for transfers between devices: 274 us -> none  [the longest x1 137 us: on_device(): lax.psum_scatter(value_terms, ('pb', 'ka'), scatter_dimension=0, tiled=True)]
    all_gather x4 -> x0, waiting for transfers between devices: 151 us -> none  [the longest x1 59.3 us: on_device(): lax.all_gather(keys, ('pb', 'ka'), axis=0, tiled=True)]
    dot_general x42 -> x0, matrix products: 81 us -> none  [the longest x1 18.9 us: make_absorb(): jnp.einsum('hgqk,khd->hgqd', weights, value_piece.astype(jnp.float32), pr...]
    all_gather x4 -> x0, blocking collectives: 71.1 us -> none  [the longest x1 28.9 us: on_device(): lax.all_gather(keys, 'pb', axis=0, tiled=True)]
    all_to_all x0 -> x2, blocking collectives: none -> 44.8 us  [exchange(): return lax.all_to_all(a, CHIPS, 0, 0, tiled=True)]
    pallas_call x0 -> x1, Pallas kernels: none -> 38.3 us  [attention(): pl.pallas_call(attention_kernel, out_shape=(jax.ShapeDtypeStruct(q.shape,...]
    reduce_sum x1, other arithmetic: 8.5 us -> 0.14 us  [on_device(): total = jnp.sum(terms.astype(F32), axis=0).astype(BF16)]
    add x4 -> x0, other arithmetic: 8.11 us -> none  [the longest x3 8.11 us: combine_partials(): earlier_sum * earlier_factor[..., None]]
  transfers between devices with their start and end apart: 6 -> 2, of which waited for: 5 -> 2; matrix products, arithmetic and copies ran while one was open for 4% -> 0% of each run, Pallas kernels for 0% -> 0%
where the time goes in v1:
time: 93.8 us; the launch traced here: 93.5 us
  blocking collectives  44.8 us (48%)
  Pallas kernels  38.3 us (41%)
  waiting for transfers between devices  5.38 us (6%)
  other arithmetic  2.43 us (3%)
  local copies, waits for them, and re-layouts  1.84 us (2%)
    all_to_all x2, blocking collectives, exchange(): return lax.all_to_all(a, CHIPS, 0, 0, tiled=True)  44.8 us
    pallas_call x1, Pallas kernels, attention(): pl.pallas_call(attention_kernel, out_shape=(jax.ShapeDtypeStruct(q.shape,...  38.3 us
    ppermute x2, waiting for transfers between devices, swap_cores(): return lax.ppermute(a, 'c', [(0, 1), (1, 0)])  5.38 us
  transfers between devices with their start and end apart: 2, of which 2 were waited for; matrix products, arithmetic and copies ran while one was open for 0% of the time, Pallas kernels for 0%

profile of v1, /device:TPU:32, one launch (start us, length us, event | category | flops | bytes accessed | tf_op | source)
XLA Modules:
  0.0 93.5 jit_solution(17907654729866517576)
XLA Ops:
  0.6 0.8 pad_maximum_fusion
  1.4 0.2 broadcast_in_dim.2
  1.6 24.0 %all_to_all.10.kva_ref = bf16[16,256,128]{2,1,0:T(8,128)(2,1)S(1)} all-to-all(bf16[16,256,128]{2,1,0:T(8,128)(2,1)S(1)} %broadcast_in_dim.2), channel_id=1, replica_groups=mesh['x'=4,'yl'=2,'yh'=2,'c'=2,'z'=8] {'x','yl','yh'}, dimensions={0} | all-to-all | bytes 2097152 | tf_op jit(solution)/shard_map/all_to_all | solution.py:142
  25.6 0.0 copy-start
  25.6 0.0 collective-permute-start
  25.6 2.7 %collective-permute-done.kvb_ref = bf16[16,256,128]{2,1,0:T(8,128)(2,1)S(1)} collective-permute-done((bf16[16,256,128]{2,1,0:T(8,128)(2,1)S(1)}, bf16[16,256,128]{2,1,0:T(8,128)(2,1)S(1)}, u32[]{:S(2)}, u32[]{:S(2)}) %collective-permute-start) | collective-permute-done | bytes 1048608 | tf_op jit(solution)/shard_map/ppermute | solution.py:138
  28.3 0.0 copy-start.1
  28.3 0.0 copy-done
  28.3 1.0 %copy-done.1 = bf16[16,256,128]{2,1,0:T(8,128)(2,1)} copy-done((bf16[16,256,128]{2,1,0:T(8,128)(2,1)}, bf16[16,256,128]{2,1,0:T(8,128)(2,1)S(1)}, u32[]{:S(2)}) %copy-start.1) | copy-done | bytes 1048600
  29.3 38.3 %shard_map.75 = (bf16[1024,128]{1,0:T(8,128)(2,1)}, bf16[1024,128]{1,0:T(8,128)(2,1)}, bf16[16,256,128]{2,1,0:T(8,128)(2,1)}, bf16[16,256,128]{2,1,0:T(8,128)(2,1)}) custom-call(bf16[1024,128]{1,0:T(8,128)(2,1)} %bitcast.12, bf16[1024,128]{1,0:T(8,128)(2,1)} %bitcast.13, bf16[16,256,128]{2,1,0:T(8,128)(2,1)} %copy-done, bf16[16,256,128]{2,1,0:T(8,128)(2,1)} %copy-done.1), custom_call_target="tpu_custom_call" | custom-call | flops 6442450944 | bytes 6291456 | tf_op jit(solution)/shard_map/pallas_call | solution.py:110
  67.6 0.1 collective-permute-start.1
  67.8 2.7 %collective-permute-done.1 = bf16[16,256,128]{2,1,0:T(8,128)(2,1)S(1)} collective-permute-done((bf16[16,256,128]{2,1,0:T(8,128)(2,1)}, bf16[16,256,128]{2,1,0:T(8,128)(2,1)S(1)}, u32[]{:S(2)}, u32[]{:S(2)}) %collective-permute-start.1) | collective-permute-done | bytes 1048608 | tf_op jit(solution)/shard_map/ppermute | solution.py:138
  70.5 1.5 %add_convert_fusion = bf16[16,256,128]{2,1,0:T(8,128)(2,1)S(1)} fusion(bf16[16,256,128]{2,1,0:T(8,128)(2,1)S(1)} %collective-permute-done.1, bf16[16,256,128]{2,1,0:T(8,128)(2,1)} %get-tuple-element.10), kind=kLoop, calls=%fused_computation | loop fusion | flops 2097152 | bytes 3145728 | tf_op jit(solution)/shard_map/convert_element_type | solution.py:153
  72.0 20.8 %all_to_all.11 = bf16[16,256,128]{2,1,0:T(8,128)(2,1)S(1)} all-to-all(bf16[16,256,128]{2,1,0:T(8,128)(2,1)S(1)} %add_convert_fusion), channel_id=1, replica_groups=mesh['x'=4,'yl'=2,'yh'=2,'c'=2,'z'=8] {'x','yl','yh'}, dimensions={0} | all-to-all | bytes 2097152 | tf_op jit(solution)/shard_map/all_to_all | solution.py:142
  92.8 0.1 reduce_sum.12
  92.9 0.6 slice_bitcast_fusion
Async XLA Ops:
  25.6 2.7 %copy-start = (bf16[16,256,128]{2,1,0:T(8,128)(2,1)}, bf16[16,256,128]{2,1,0:T(8,128)(2,1)S(1)}, u32[]{:S(2)}) copy-start(bf16[16,256,128]{2,1,0:T(8,128)(2,1)S(1)} %all_to_all.10.kva_ref) | copy-start | bytes 3145732
  25.6 2.7 %collective-permute-start = (bf16[16,256,128]{2,1,0:T(8,128)(2,1)S(1)}, bf16[16,256,128]{2,1,0:T(8,128)(2,1)S(1)}, u32[]{:S(2)}, u32[]{:S(2)}) collective-permute-start(bf16[16,256,128]{2,1,0:T(8,128)(2,1)S(1)} %all_to_all.10.kva_ref), channel_id=1, source_target_pairs={{0,8},{8,0},{1,9},{9,1},{2,10},{10,2},{3,11},{11,3},{4,12},{12,4},... | collective-permute-start | bytes 3145736 | tf_op jit(solution)/shard_map/ppermute | solution.py:138
  28.3 1.0 %copy-start.1 = (bf16[16,256,128]{2,1,0:T(8,128)(2,1)}, bf16[16,256,128]{2,1,0:T(8,128)(2,1)S(1)}, u32[]{:S(2)}) copy-start(bf16[16,256,128]{2,1,0:T(8,128)(2,1)S(1)} %collective-permute-done.kvb_ref) | copy-start | bytes 3145732
  67.6 2.9 %collective-permute-start.1 = (bf16[16,256,128]{2,1,0:T(8,128)(2,1)}, bf16[16,256,128]{2,1,0:T(8,128)(2,1)S(1)}, u32[]{:S(2)}, u32[]{:S(2)}) collective-permute-start(bf16[16,256,128]{2,1,0:T(8,128)(2,1)} %get-tuple-element.11), channel_id=1, source_target_pairs={{0,8},{8,0},{1,9},{9,1},{2,10},{10,2},{3,11},{11,3},{4,12},{12,4},... | collective-permute-start | bytes 3145736 | tf_op jit(solution)/shard_map/ppermute | solution.py:138

commit v2 on v1

v2 whole, which is shorter than its diff:
```python
import functools
import math

import jax
import jax.numpy as jnp
from jax import lax
from jax.experimental import pallas as pl
from jax.experimental.pallas import tpu as pltpu
from jax.sharding import Mesh, PartitionSpec as P

HEAD_DIM = 128
SCALE = HEAD_DIM ** (-0.5)
EXP2_SCALE = SCALE * math.log2(math.e)
CHIPS = ("x", "yl", "yh")
NCHIP = 16
ROWS = 128
QB = 256
KA = 1024
KB = 512
F32 = jnp.float32
BF16 = jnp.bfloat16


def dot(a, b):
    return jnp.dot(a, b, preferred_element_type=F32)


def dot_t(a, b):
    return lax.dot_general(a, b, (((1,), (1,)), ((), ())), preferred_element_type=F32)


def attention_kernel(q_ref, g_ref, kva_ref, kvb_ref, out_ref, dq_ref, da_ref, db_ref, *f32_scratch):
    rows = q_ref.shape[0]
    total = 2 * NCHIP * ROWS
    pl.run_scoped(
        functools.partial(
            attention_body, q_ref, g_ref, kva_ref, kvb_ref, out_ref, dq_ref, da_ref, db_ref, *f32_scratch
        ),
        pltpu.VMEM((rows, HEAD_DIM), BF16),
        pltpu.VMEM((total, HEAD_DIM), BF16),
        pltpu.VMEM((total, HEAD_DIM), BF16),
        pltpu.VMEM((HEAD_DIM, total), BF16),
        pltpu.VMEM((HEAD_DIM + 16, total), BF16),
        pltpu.VMEM((total, rows), BF16),
        pltpu.VMEM((KB, rows), BF16),
        pltpu.VMEM((KB, rows), BF16),
        pltpu.VMEM((rows, HEAD_DIM), BF16),
    )


def attention_body(
    q_ref, g_ref, kva_ref, kvb_ref,
    out_ref, dq_ref, da_ref, db_ref,
    s0, s1, acc, d_buf, dqt,
    q_all, k_all, v_all, kt, vt, p_buf, ds0, ds1, gn_buf,
):
    rows = q_ref.shape[0]
    total = k_all.shape[0]
    nq = rows // QB
    per = KB // ROWS
    chunks = total // KB

    def span(b):
        return slice(b * QB, (b + 1) * QB)

    q_all[...] = q_ref[...]
    vt[HEAD_DIM:, :] = jnp.ones((vt.shape[0] - HEAD_DIM, total), BF16)
    for half, ref in enumerate((kva_ref, kvb_ref)):
        def spread(i, carry, half=half, ref=ref):
            for j in range(4):
                b = i * 4 + j
                col = pl.multiple_of((half * NCHIP + b) * ROWS, ROWS)
                k = ref[b, :ROWS, :]
                v = ref[b, ROWS:, :]
                k_all[pl.ds(col, ROWS), :] = k
                v_all[pl.ds(col, ROWS), :] = v
                kt[:, pl.ds(col, ROWS)] = jnp.transpose(k)
                vt[:HEAD_DIM, pl.ds(col, ROWS)] = jnp.transpose(v)
            return carry
        lax.fori_loop(0, NCHIP // 4, spread, 0)

    def finish(b):
        qs = span(b)
        inv = 1.0 / acc[HEAD_DIM:HEAD_DIM + 1, :]
        out_t = acc[:HEAD_DIM, :] * inv
        out_ref[qs, :] = jnp.transpose(out_t).astype(BF16)
        inv_rows = jnp.transpose(jnp.broadcast_to(inv, (HEAD_DIM, QB)))
        gn = (g_ref[qs, :].astype(F32) * inv_rows).astype(BF16)
        gn_buf[qs, :] = gn
        gn_t = jnp.transpose(gn.astype(F32))
        d_buf[:, qs] = jnp.broadcast_to(jnp.sum(gn_t * out_t, axis=0, keepdims=True), (8, QB))

    s_bufs = (s0, s1)
    peak = None
    for stage in range(nq + 1):
        new = stage if stage < nq else None
        old = stage - 1 if stage > 0 else None
        if old is not None:
            acc[...] = jnp.zeros_like(acc)

        def forward(c, top, new=new, old=old, peak=peak):
            row = pl.multiple_of(c * KA, KA)
            if new is not None:
                s = dot_t(k_all[pl.ds(row, KA), :], q_all[span(new), :])
                s_bufs[new % 2][pl.ds(row, KA), :] = s
                top = jnp.maximum(top, jnp.max(s.reshape(KA // 8, 8, QB), axis=0))
            if old is not None:
                p = jnp.exp2(s_bufs[old % 2][pl.ds(row, KA), :] * EXP2_SCALE - peak).astype(BF16)
                p_buf[pl.ds(row, KA), span(old)] = p
                acc[...] += dot(vt[:, pl.ds(row, KA)], p)
            return top
        top = lax.fori_loop(0, total // KA, forward, jnp.full((8, QB), -jnp.inf, F32))
        if old is not None:
            finish(old)
        peak = jnp.max(top, axis=0, keepdims=True) * EXP2_SCALE

    dqt[...] = jnp.zeros_like(dqt)
    ds_bufs = (ds0, ds1)

    def score_grad(c, b):
        keys, qs = slice(c * KB, (c + 1) * KB), span(b)
        dp = dot_t(v_all[keys, :], gn_buf[qs, :])
        ds_bufs[c % 2][:, qs] = (p_buf[keys, qs].astype(F32) * (dp - d_buf[0:1, qs])).astype(BF16)

    def store(c, part, lo, value):
        ref = (da_ref, db_ref)[c * per // NCHIP]
        first = (c * per) % NCHIP + lo // ROWS
        n = value.shape[0] // ROWS
        ref[first:first + n, part * ROWS:(part + 1) * ROWS, :] = value.astype(BF16).reshape(n, ROWS, HEAD_DIM)

    def value_grad(c, lo):
        store(c, 1, lo, dot(p_buf[c * KB + lo:c * KB + lo + KB // 2, :], gn_buf[...]))

    def key_grad(c, lo):
        store(c, 0, lo, dot(ds_bufs[c % 2][lo:lo + KB // 2, :], q_all[...]) * SCALE)

    def query_grad(c, b):
        dqt[:, span(b)] += dot(kt[:, c * KB:(c + 1) * KB], ds_bufs[c % 2][:, span(b)])

    for c in range(chunks + 1):
        prior = c - 1
        for b in range(nq):
            if c < chunks:
                score_grad(c, b)
            if prior >= 0:
                if b == 0:
                    value_grad(prior, 0)
                    value_grad(prior, KB // 2)
                elif b == 1:
                    key_grad(prior, 0)
                    key_grad(prior, KB // 2)
                else:
                    query_grad(prior, 2 * b - 4)
                    query_grad(prior, 2 * b - 3)
    for b in range(nq):
        dq_ref[span(b), :] = (jnp.transpose(dqt[:, span(b)]) * SCALE).astype(BF16)


def attention(q, g, kva, kvb):
    rows = q.shape[0]
    total = 2 * NCHIP * ROWS
    vmem = pl.BlockSpec(memory_space=pltpu.VMEM)
    return pl.pallas_call(
        attention_kernel,
        out_shape=(
            jax.ShapeDtypeStruct(q.shape, BF16),
            jax.ShapeDtypeStruct(q.shape, BF16),
            jax.ShapeDtypeStruct(kva.shape, BF16),
            jax.ShapeDtypeStruct(kvb.shape, BF16),
        ),
        in_specs=[vmem] * 4,
        out_specs=(vmem,) * 4,
        scratch_shapes=[
            pltpu.VMEM((total, QB), F32),
            pltpu.VMEM((total, QB), F32),
            pltpu.VMEM((HEAD_DIM + 16, QB), F32),
            pltpu.VMEM((8, rows), F32),
            pltpu.VMEM((HEAD_DIM, rows), F32),
        ],
        cost_estimate=pl.CostEstimate(
            flops=12 * rows * total * HEAD_DIM, transcendentals=rows * total, bytes_accessed=6 << 20
        ),
        compiler_params=pltpu.CompilerParams(vmem_limit_bytes=56 << 20),
    )(q, g, kva, kvb)


def swap_cores(a):
    return lax.ppermute(a, "c", [(0, 1), (1, 0)])


def exchange(a):
    return lax.all_to_all(a, CHIPS, 0, 0, tiled=True)


def on_device(queries, keys, values, out_grad):
    kv = jnp.concatenate([keys[:, 0, :], values[:, 0, :]], axis=0)
    kva = exchange(jnp.broadcast_to(kv[None], (NCHIP,) + kv.shape))
    kvb = swap_cores(kva)
    q = queries.reshape(-1, HEAD_DIM)
    g = out_grad.reshape(-1, HEAD_DIM)
    out, dq, da, db = attention(q, g, kva, kvb)
    mine = swap_cores(db)
    terms = exchange((da.astype(F32) + mine.astype(F32)).astype(BF16))
    total = jnp.sum(terms.astype(F32), axis=0).astype(BF16)
    return (
        out.reshape(queries.shape),
        dq.reshape(queries.shape),
        total[:ROWS].reshape(keys.shape),
        total[ROWS:].reshape(values.shape),
    )


def solution(mesh):
    fine = Mesh(mesh.devices.reshape(4, 2, 2, 2, 8), CHIPS + ("c", "z"))
    spec = P(CHIPS + ("c",), "z", None)
    return jax.shard_map(
        on_device,
        mesh=fine,
        in_specs=(spec,) * 4,
        out_specs=(spec,) * 4,
        check_vma=False,
    )
```

time: 93.8 us -> 75.5 us (0.80)
  Pallas kernels: 38.3 us -> 20 us
    pallas_call x1, Pallas kernels: 38.3 us -> 20 us  [attention(): pl.pallas_call(attention_kernel, out_shape=(jax.ShapeDtypeStruct(q.shape,...]
where the time goes in v2:
time: 75.5 us; the launch traced here: 75.2 us
  blocking collectives  44.8 us (59%)
  Pallas kernels  20 us (26%)
  waiting for transfers between devices  5.36 us (7%)
  other arithmetic  2.43 us (3%)
  local copies, waits for them, and re-layouts  1.84 us (2%)
    all_to_all x2, blocking collectives, exchange(): return lax.all_to_all(a, CHIPS, 0, 0, tiled=True)  44.8 us
    pallas_call x1, Pallas kernels, attention(): pl.pallas_call(attention_kernel, out_shape=(jax.ShapeDtypeStruct(q.shape,...  20 us
    ppermute x2, waiting for transfers between devices, swap_cores(): return lax.ppermute(a, 'c', [(0, 1), (1, 0)])  5.36 us
  transfers between devices with their start and end apart: 2, of which 2 were waited for; matrix products, arithmetic and copies ran while one was open for 0% of the time, Pallas kernels for 0%

profile of v2, /device:TPU:32, one launch (start us, length us, event | category | flops | bytes accessed | tf_op | source)
XLA Modules:
  0.0 75.2 jit_solution(8294515749719677962)
XLA Ops:
  0.6 0.8 %pad_maximum_fusion = bf16[256,128]{1,0:T(8,128)(2,1)S(1)} fusion(bf16[128,128]{1,0:T(8,128)(2,1)} %bitcast.10, bf16[128,128]{1,0:T(8,128)(2,1)} %bitcast.11), kind=kLoop, calls=%fused_computation.1 | loop fusion | flops 131072 | bytes 131072 | tf_op jit(solution)/shard_map/concatenate | solution.py:196
  1.4 0.2 broadcast_in_dim.2
  1.6 24.0 %all_to_all.10.kva_ref = bf16[16,256,128]{2,1,0:T(8,128)(2,1)S(1)} all-to-all(bf16[16,256,128]{2,1,0:T(8,128)(2,1)S(1)} %broadcast_in_dim.2), channel_id=1, replica_groups=mesh['x'=4,'yl'=2,'yh'=2,'c'=2,'z'=8] {'x','yl','yh'}, dimensions={0} | all-to-all | bytes 2097152 | tf_op jit(solution)/shard_map/all_to_all | solution.py:192
  25.6 0.0 copy-start
  25.6 0.0 collective-permute-start
  25.6 2.7 %collective-permute-done.kvb_ref = bf16[16,256,128]{2,1,0:T(8,128)(2,1)S(1)} collective-permute-done((bf16[16,256,128]{2,1,0:T(8,128)(2,1)S(1)}, bf16[16,256,128]{2,1,0:T(8,128)(2,1)S(1)}, u32[]{:S(2)}, u32[]{:S(2)}) %collective-permute-start) | collective-permute-done | bytes 1048608 | tf_op jit(solution)/shard_map/ppermute | solution.py:188
  28.3 0.0 copy-start.1
  28.3 0.0 copy-done
  28.3 1.0 %copy-done.1 = bf16[16,256,128]{2,1,0:T(8,128)(2,1)} copy-done((bf16[16,256,128]{2,1,0:T(8,128)(2,1)}, bf16[16,256,128]{2,1,0:T(8,128)(2,1)S(1)}, u32[]{:S(2)}) %copy-start.1) | copy-done | bytes 1048600
  29.3 20.0 %shard_map.75 = (bf16[1024,128]{1,0:T(8,128)(2,1)}, bf16[1024,128]{1,0:T(8,128)(2,1)}, bf16[16,256,128]{2,1,0:T(8,128)(2,1)}, bf16[16,256,128]{2,1,0:T(8,128)(2,1)}) custom-call(bf16[1024,128]{1,0:T(8,128)(2,1)} %bitcast.12, bf16[1024,128]{1,0:T(8,128)(2,1)} %bitcast.13, bf16[16,256,128]{2,1,0:T(8,128)(2,1)} %copy-done, bf16[16,256,128]{2,1,0:T(8,128)(2,1)} %copy-done.1), custom_call_target="tpu_custom_call" | custom-call | flops 6442450944 | bytes 6291456 | tf_op jit(solution)/shard_map/pallas_call | solution.py:163
  49.3 0.2 collective-permute-start.1
  49.4 2.7 %collective-permute-done.1 = bf16[16,256,128]{2,1,0:T(8,128)(2,1)S(1)} collective-permute-done((bf16[16,256,128]{2,1,0:T(8,128)(2,1)}, bf16[16,256,128]{2,1,0:T(8,128)(2,1)S(1)}, u32[]{:S(2)}, u32[]{:S(2)}) %collective-permute-start.1) | collective-permute-done | bytes 1048608 | tf_op jit(solution)/shard_map/ppermute | solution.py:188
  52.1 1.5 %add_convert_fusion = bf16[16,256,128]{2,1,0:T(8,128)(2,1)S(1)} fusion(bf16[16,256,128]{2,1,0:T(8,128)(2,1)S(1)} %collective-permute-done.1, bf16[16,256,128]{2,1,0:T(8,128)(2,1)} %get-tuple-element.10), kind=kLoop, calls=%fused_computation | loop fusion | flops 2097152 | bytes 3145728 | tf_op jit(solution)/shard_map/convert_element_type | solution.py:203
  53.6 20.8 %all_to_all.11 = bf16[16,256,128]{2,1,0:T(8,128)(2,1)S(1)} all-to-all(bf16[16,256,128]{2,1,0:T(8,128)(2,1)S(1)} %add_convert_fusion), channel_id=1, replica_groups=mesh['x'=4,'yl'=2,'yh'=2,'c'=2,'z'=8] {'x','yl','yh'}, dimensions={0} | all-to-all | bytes 2097152 | tf_op jit(solution)/shard_map/all_to_all | solution.py:192
  74.4 0.1 reduce_sum.12
  74.6 0.6 slice_bitcast_fusion
Async XLA Ops:
  25.6 2.7 %copy-start = (bf16[16,256,128]{2,1,0:T(8,128)(2,1)}, bf16[16,256,128]{2,1,0:T(8,128)(2,1)S(1)}, u32[]{:S(2)}) copy-start(bf16[16,256,128]{2,1,0:T(8,128)(2,1)S(1)} %all_to_all.10.kva_ref) | copy-start | bytes 3145732
  25.6 2.7 %collective-permute-start = (bf16[16,256,128]{2,1,0:T(8,128)(2,1)S(1)}, bf16[16,256,128]{2,1,0:T(8,128)(2,1)S(1)}, u32[]{:S(2)}, u32[]{:S(2)}) collective-permute-start(bf16[16,256,128]{2,1,0:T(8,128)(2,1)S(1)} %all_to_all.10.kva_ref), channel_id=1, source_target_pairs={{0,8},{8,0},{1,9},{9,1},{2,10},{10,2},{3,11},{11,3},{4,12},{12,4},... | collective-permute-start | bytes 3145736 | tf_op jit(solution)/shard_map/ppermute | solution.py:188
  28.3 1.0 %copy-start.1 = (bf16[16,256,128]{2,1,0:T(8,128)(2,1)}, bf16[16,256,128]{2,1,0:T(8,128)(2,1)S(1)}, u32[]{:S(2)}) copy-start(bf16[16,256,128]{2,1,0:T(8,128)(2,1)S(1)} %collective-permute-done.kvb_ref) | copy-start | bytes 3145732
  49.3 2.9 %collective-permute-start.1 = (bf16[16,256,128]{2,1,0:T(8,128)(2,1)}, bf16[16,256,128]{2,1,0:T(8,128)(2,1)S(1)}, u32[]{:S(2)}, u32[]{:S(2)}) collective-permute-start(bf16[16,256,128]{2,1,0:T(8,128)(2,1)} %get-tuple-element.11), channel_id=1, source_target_pairs={{0,8},{8,0},{1,9},{9,1},{2,10},{10,2},{3,11},{11,3},{4,12},{12,4},... | collective-permute-start | bytes 3145736 | tf_op jit(solution)/shard_map/ppermute | solution.py:188

commit v3 on v1

v3 whole, which is shorter than its diff:
```python
import math

import jax
import jax.numpy as jnp
from jax import lax
from jax.experimental import pallas as pl
from jax.experimental.pallas import tpu as pltpu
from jax.sharding import Mesh, PartitionSpec as P

HEAD_DIM = 128
SCALE = HEAD_DIM ** (-0.5)
EXP2_SCALE = SCALE * math.log2(math.e)
LOG2E = math.log2(math.e)
CHIPS = ("x", "yl", "yh")
NCHIP = 16
ROWS = 128
KEYS = NCHIP * ROWS
QB = 256
KB = 512
VMEM_LIMIT = 32 << 20
F32 = jnp.float32
BF16 = jnp.bfloat16


def dot(a, b):
    return jnp.dot(a, b, preferred_element_type=F32)


def dot_t(a, b):
    return lax.dot_general(a, b, (((1,), (1,)), ((), ())), preferred_element_type=F32)


def span(b):
    return slice(b * QB, (b + 1) * QB)


def as_rows(line):
    return jnp.transpose(jnp.broadcast_to(line, (HEAD_DIM, line.shape[1])))


def forward_kernel(q_ref, q2_ref, g_ref, g2_ref, kv_ref, stat_ref, own_ref, send_ref, s0, s1):
    own_rows = q_ref.shape[0]
    rows = 2 * own_rows

    def body(q_all, k_all, vt):
        q_all[:own_rows, :] = q_ref[...]
        q_all[own_rows:, :] = q2_ref[...]
        vt[HEAD_DIM:, :] = jnp.ones((vt.shape[0] - HEAD_DIM, KEYS), BF16)
        for b in range(NCHIP):
            block = slice(b * ROWS, (b + 1) * ROWS)
            k_all[block, :] = kv_ref[b, :ROWS, :]
            vt[:HEAD_DIM, block] = jnp.transpose(kv_ref[b, ROWS:, :])
        stat_ref[...] = jnp.zeros_like(stat_ref)

        def finish(b, acc, peak):
            qs = span(b)
            total = acc[HEAD_DIM:HEAD_DIM + 1, :]
            out_t = acc[:HEAD_DIM, :] * (1.0 / total)
            half, lo = divmod(b * QB, own_rows)
            local = slice(lo, lo + QB)
            grad_t = jnp.transpose((g_ref, g2_ref)[half][local, :].astype(F32))
            stat_ref[0:1, qs] = peak
            stat_ref[1:2, qs] = total
            stat_ref[2:3, qs] = jnp.sum(grad_t * out_t, axis=0, keepdims=True)
            out = jnp.transpose(out_t)
            if half == 0:
                own_ref[local, :] = out
            else:
                send_ref[local, :] = out.astype(BF16)

        s_bufs = (s0, s1)
        peak = None
        for stage in range(rows // QB + 1):
            old_peak = peak
            if stage < rows // QB:
                s = dot_t(k_all[...], q_all[span(stage), :])
                s_bufs[stage % 2][...] = s
                top = jnp.max(s.reshape(KEYS // 8, 8, QB), axis=0)
                peak = jnp.max(top, axis=0, keepdims=True) * EXP2_SCALE
            if stage > 0:
                b = stage - 1
                p = jnp.exp2(s_bufs[b % 2][...] * EXP2_SCALE - old_peak).astype(BF16)
                finish(b, dot(vt[...], p), old_peak)

    pl.run_scoped(
        body,
        pltpu.VMEM((rows, HEAD_DIM), BF16),
        pltpu.VMEM((KEYS, HEAD_DIM), BF16),
        pltpu.VMEM((HEAD_DIM + 16, KEYS), BF16),
    )


def backward_kernel(
    q_ref, q2_ref, g_ref, g2_ref, kv_ref, stat_ref, stat2_ref, own_ref, recv_ref,
    out_ref, dq_ref, send_ref, dkv_ref,
    lse, dots, dqt,
):
    own_rows = q_ref.shape[0]
    rows = 2 * own_rows
    nq = rows // QB
    per = KB // ROWS
    chunks = KEYS // KB

    def body(q_all, g_all, k_all, v_all, kt, p0, p1, ds0, ds1):
        q_all[:own_rows, :] = q_ref[...]
        q_all[own_rows:, :] = q2_ref[...]
        g_all[:own_rows, :] = g_ref[...]
        g_all[own_rows:, :] = g2_ref[...]
        for b in range(NCHIP):
            block = slice(b * ROWS, (b + 1) * ROWS)
            k = kv_ref[b, :ROWS, :]
            k_all[block, :] = k
            v_all[block, :] = kv_ref[b, ROWS:, :]
            kt[:, block] = jnp.transpose(k)

        for half in range(2):
            here = slice(half * own_rows, (half + 1) * own_rows)
            there = slice((1 - half) * own_rows, (2 - half) * own_rows)
            peak_a, peak_b = stat_ref[0:1, here], stat2_ref[0:1, there]
            peak = jnp.maximum(peak_a, peak_b)
            total_a = stat_ref[1:2, here] * jnp.exp2(peak_a - peak)
            total_b = stat2_ref[1:2, there] * jnp.exp2(peak_b - peak)
            total = total_a + total_b
            weight_a, weight_b = total_a / total, total_b / total
            lse[:, here] = jnp.broadcast_to(peak + jnp.log(total) * LOG2E, (8, own_rows))
            dots[:, here] = jnp.broadcast_to(
                weight_a * stat_ref[2:3, here] + weight_b * stat2_ref[2:3, there], (8, own_rows)
            )
            if half == 0:
                for lo in range(0, own_rows, QB):
                    local = slice(lo, lo + QB)
                    out_ref[local, :] = (
                        own_ref[local, :] * as_rows(weight_a[:, local])
                        + recv_ref[local, :].astype(F32) * as_rows(weight_b[:, local])
                    ).astype(BF16)

        dqt[...] = jnp.zeros_like(dqt)
        p_bufs, ds_bufs = (p0, p1), (ds0, ds1)

        def score_grad(c, b):
            keys, qs = slice(c * KB, (c + 1) * KB), span(b)
            s = dot_t(k_all[keys, :], q_all[qs, :])
            dp = dot_t(v_all[keys, :], g_all[qs, :])
            p = jnp.exp2(s * EXP2_SCALE - lse[0:1, qs])
            p_bufs[c % 2][:, qs] = p.astype(BF16)
            ds_bufs[c % 2][:, qs] = (p * (dp - dots[0:1, qs])).astype(BF16)

        def store(c, part, lo, value):
            first = c * per + lo // ROWS
            n = value.shape[0] // ROWS
            dkv_ref[first:first + n, part * ROWS:(part + 1) * ROWS, :] = value.astype(BF16).reshape(
                n, ROWS, HEAD_DIM
            )

        def value_grad(c, lo):
            store(c, 1, lo, dot(p_bufs[c % 2][lo:lo + KB // 2, :], g_all[...]))

        def key_grad(c, lo):
            store(c, 0, lo, dot(ds_bufs[c % 2][lo:lo + KB // 2, :], q_all[...]) * SCALE)

        def query_grad(c, b):
            dqt[:, span(b)] += dot(kt[:, c * KB:(c + 1) * KB], ds_bufs[c % 2][:, span(b)])

        for c in range(chunks + 1):
            prior = c - 1
            for b in range(nq):
                if c < chunks:
                    score_grad(c, b)
                if prior >= 0:
                    if b < 2:
                        value_grad(prior, b * (KB // 2))
                    elif b < 4:
                        key_grad(prior, (b - 2) * (KB // 2))
                    else:
                        query_grad(prior, 2 * b - 8)
                        query_grad(prior, 2 * b - 7)
        for b in range(nq):
            half, lo = divmod(b * QB, own_rows)
            (dq_ref, send_ref)[half][lo:lo + QB, :] = jnp.transpose(dqt[:, span(b)]) * SCALE

    pl.run_scoped(
        body,
        pltpu.VMEM((rows, HEAD_DIM), BF16),
        pltpu.VMEM((rows, HEAD_DIM), BF16),
        pltpu.VMEM((KEYS, HEAD_DIM), BF16),
        pltpu.VMEM((KEYS, HEAD_DIM), BF16),
        pltpu.VMEM((HEAD_DIM, KEYS), BF16),
        *[pltpu.VMEM((KB, rows), BF16) for _ in range(4)],
    )


def forward(q, q2, g, g2, kv):
    n = q.shape[0]
    vmem = pl.BlockSpec(memory_space=pltpu.VMEM)
    return pl.pallas_call(
        forward_kernel,
        out_shape=(
            jax.ShapeDtypeStruct((8, 2 * n), F32),
            jax.ShapeDtypeStruct(q.shape, F32),
            jax.ShapeDtypeStruct(q.shape, BF16),
        ),
        in_specs=[vmem] * 5,
        out_specs=(vmem,) * 3,
        scratch_shapes=[pltpu.VMEM((KEYS, QB), F32), pltpu.VMEM((KEYS, QB), F32)],
        cost_estimate=pl.CostEstimate(
            flops=8 * n * KEYS * HEAD_DIM, transcendentals=2 * n * KEYS, bytes_accessed=3 << 20
        ),
        compiler_params=pltpu.CompilerParams(vmem_limit_bytes=VMEM_LIMIT),
    )(q, q2, g, g2, kv)


def backward(q, q2, g, g2, kv, stat, stat2, own, recv):
    n = q.shape[0]
    vmem = pl.BlockSpec(memory_space=pltpu.VMEM)
    return pl.pallas_call(
        backward_kernel,
        out_shape=(
            jax.ShapeDtypeStruct(q.shape, BF16),
            jax.ShapeDtypeStruct(q.shape, F32),
            jax.ShapeDtypeStruct(q.shape, F32),
            jax.ShapeDtypeStruct(kv.shape, BF16),
        ),
        in_specs=[vmem] * 9,
        out_specs=(vmem,) * 4,
        scratch_shapes=[
            pltpu.VMEM((8, 2 * n), F32),
            pltpu.VMEM((8, 2 * n), F32),
            pltpu.VMEM((HEAD_DIM, 2 * n), F32),
        ],
        cost_estimate=pl.CostEstimate(
            flops=20 * n * KEYS * HEAD_DIM, transcendentals=2 * n * KEYS, bytes_accessed=5 << 20
        ),
        compiler_params=pltpu.CompilerParams(vmem_limit_bytes=VMEM_LIMIT),
    )(q, q2, g, g2, kv, stat, stat2, own, recv)


def swap_cores(a):
    return lax.ppermute(a, "c", [(0, 1), (1, 0)])


def exchange(a):
    return lax.all_to_all(a, CHIPS, 0, 0, tiled=True)


def on_device(queries, keys, values, out_grad):
    q = queries.reshape(-1, HEAD_DIM)
    g = out_grad.reshape(-1, HEAD_DIM)
    q2, g2 = swap_cores(q), swap_cores(g)
    kv = jnp.concatenate([keys[:, 0, :], values[:, 0, :]], axis=0)
    kv = exchange(jnp.broadcast_to(kv[None], (NCHIP,) + kv.shape))
    stat, own, send = forward(q, q2, g, g2, kv)
    stat2, recv = swap_cores(stat), swap_cores(send)
    out, dq, dq_send, dkv = backward(q, q2, g, g2, kv, stat, stat2, own, recv)
    terms = exchange(dkv)
    dq = (dq + swap_cores(dq_send)).astype(BF16)
    total = jnp.sum(terms.astype(F32), axis=0).astype(BF16)
    return (
        out.reshape(queries.shape),
        dq.reshape(queries.shape),
        total[:ROWS].reshape(keys.shape),
        total[ROWS:].reshape(values.shape),
    )


def solution(mesh):
    fine = Mesh(mesh.devices.reshape(4, 2, 2, 2, 8), CHIPS + ("c", "z"))
    spec = P(CHIPS + ("c",), "z", None)
    return jax.shard_map(
        on_device,
        mesh=fine,
        in_specs=(spec,) * 4,
        out_specs=(spec,) * 4,
        check_vma=False,
    )
```

time: 93.8 us -> 72.1 us (0.77)
  blocking collectives: 44.8 us -> 0 us
  waiting for transfers between devices: 5.38 us -> 36.7 us
  Pallas kernels: 38.3 us -> 17.3 us
  starting transfers between devices: 0.15 us -> 13.2 us
    all_to_all x2 -> x0, blocking collectives: 44.8 us -> none  [exchange(): return lax.all_to_all(a, CHIPS, 0, 0, tiled=True)]
    all_to_all x0 -> x2, waiting for transfers between devices: none -> 32.3 us  [exchange(): return lax.all_to_all(a, CHIPS, 0, 0, tiled=True)]
    pallas_call x1 -> x2, Pallas kernels: 38.3 us -> 17.3 us  [the longest x1 10.9 us: backward(): pl.pallas_call(backward_kernel, out_shape=(jax.ShapeDtypeStruct(q.shape,...]
    all_to_all x0 -> x2, starting transfers between devices: none -> 11.9 us  [exchange(): return lax.all_to_all(a, CHIPS, 0, 0, tiled=True)]
    convert_element_type x1 -> x0, other arithmetic: 1.5 us -> none  [on_device(): terms = exchange((da.astype(F32) + mine.astype(F32)).astype(BF16))]
    ppermute x2 -> x5, starting transfers between devices: 0.15 us -> 1.26 us  [swap_cores(): return lax.ppermute(a, 'c', [(0, 1), (1, 0)])]
    unnamed x4, local copies, waits for them, and re-layouts: 1.02 us -> 0.01 us
    broadcast_in_dim x1, local copies, waits for them, and re-layouts: 0.19 us -> 1.17 us  [on_device(): kv = exchange(jnp.broadcast_to(kv[None], (NCHIP,) + kv.shape))]
  transfers between devices with their start and end apart: 2 -> 7, of which waited for: 2 -> 6; matrix products, arithmetic and copies ran while one was open for 0% -> 1% of each run, Pallas kernels for 0% -> 0%
where the time goes in v3:
time: 72.1 us; the launch traced here: 71.4 us
  waiting for transfers between devices  36.7 us (51%)
  Pallas kernels  17.3 us (24%)
  starting transfers between devices  13.2 us (18%)
  local copies, waits for them, and re-layouts  1.81 us (3%)
  other arithmetic  1.71 us (2%)
    all_to_all x2, waiting for transfers between devices, exchange(): return lax.all_to_all(a, CHIPS, 0, 0, tiled=True)  32.3 us
    all_to_all x2, starting transfers between devices, exchange(): return lax.all_to_all(a, CHIPS, 0, 0, tiled=True)  11.9 us
    pallas_call x1, Pallas kernels, backward(): pl.pallas_call(backward_kernel, out_shape=(jax.ShapeDtypeStruct(q.shape,...  10.9 us
    pallas_call x1, Pallas kernels, forward(): pl.pallas_call(forward_kernel, out_shape=(jax.ShapeDtypeStruct((8, 2 * n)...  6.38 us
    ppermute x5, waiting for transfers between devices, swap_cores(): return lax.ppermute(a, 'c', [(0, 1), (1, 0)])  4.41 us
  transfers between devices with their start and end apart: 7, of which 6 were waited for; matrix products, arithmetic and copies ran while one was open for 1% of the time, Pallas kernels for 0%

profile of v3, /device:TPU:32, one launch (start us, length us, event | category | flops | bytes accessed | tf_op | source)
XLA Modules:
  0.0 71.4 jit_solution(5557724370382723487)
XLA Ops:
  0.6 0.8 %pad_maximum_fusion = bf16[256,128]{1,0:T(8,128)(2,1)S(1)} fusion(bf16[128,128]{1,0:T(8,128)(2,1)} %bitcast.17, bf16[128,128]{1,0:T(8,128)(2,1)} %bitcast.18), kind=kLoop, calls=%fused_computation.2 | loop fusion | flops 131072 | bytes 131072 | tf_op jit(solution)/shard_map/concatenate | solution.py:249
  1.4 1.2 %broadcast_in_dim.2 = bf16[16,256,128]{2,1,0:T(8,128)(2,1)} broadcast(bf16[256,128]{1,0:T(8,128)(2,1)S(1)} %pad_maximum_fusion), dimensions={1,2} | broadcast | bytes 1114112 | tf_op jit(solution)/shard_map/broadcast_in_dim | solution.py:250
  2.6 0.0 copy-start
  2.6 0.0 copy-start.1
  2.6 7.2 %all-to-all-start = ((bf16[16,256,128]{2,1,0:T(8,128)(2,1)}), bf16[16,256,128]{2,1,0:T(8,128)(2,1)S(1)}, u32[]{:S(2)}, u32[]{:S(2)}) async-start(bf16[16,256,128]{2,1,0:T(8,128)(2,1)} %broadcast_in_dim.2), calls=%async_computation | async-start | bytes 2097152 | tf_op jit(solution)/shard_map/all_to_all | solution.py:242
  9.8 0.0 copy-done
  9.8 0.1 collective-permute-start
  9.9 0.0 copy-done.1
  9.9 0.5 collective-permute-start.1
  10.4 1.0 %collective-permute-done.q2_ref = bf16[1024,128]{1,0:T(8,128)(2,1)S(1)} collective-permute-done((bf16[1024,128]{1,0:T(8,128)(2,1)S(1)}, bf16[1024,128]{1,0:T(8,128)(2,1)S(1)}, u32[]{:S(2)}, u32[]{:S(2)}) %collective-permute-start) | collective-permute-done | bytes 262176 | tf_op jit(solution)/shard_map/ppermute | solution.py:238
  11.4 0.4 collective-permute-done.1.g2_ref
  11.8 16.2 %all-to-all-done.kv_ref = bf16[16,256,128]{2,1,0:T(8,128)(2,1)S(1)} async-done(((bf16[16,256,128]{2,1,0:T(8,128)(2,1)}), bf16[16,256,128]{2,1,0:T(8,128)(2,1)S(1)}, u32[]{:S(2)}, u32[]{:S(2)}) %all-to-all-start) | async-done | bytes 1048608 | tf_op jit(solution)/shard_map/all_to_all | solution.py:242
  28.0 6.4 %shard_map.75 = (f32[8,2048]{1,0:T(8,128)S(1)}, f32[1024,128]{1,0:T(8,128)S(1)}, bf16[1024,128]{1,0:T(8,128)(2,1)S(1)}) custom-call(bf16[1024,128]{1,0:T(8,128)(2,1)S(1)} %bitcast.12, bf16[1024,128]{1,0:T(8,128)(2,1)S(1)} %collective-permute-done.q2_ref, bf16[1024,128]{1,0:T(8,128)(2,1)S(1)} %bitcast.15, ...), custom_call_target="tpu_custom_call" | custom-call | flops 2147483648 | bytes 3145728 | tf_op jit(solution)/shard_map/pallas_call | solution.py:195
  34.3 0.1 collective-permute-start.3
  34.4 0.5 collective-permute-start.2
  34.9 1.1 %collective-permute-done.2.stat2_ref = f32[8,2048]{1,0:T(8,128)S(1)} collective-permute-done((f32[8,2048]{1,0:T(8,128)S(1)}, f32[8,2048]{1,0:T(8,128)S(1)}, u32[]{:S(2)}, u32[]{:S(2)}) %collective-permute-start.2) | collective-permute-done | bytes 65568 | tf_op jit(solution)/shard_map/ppermute | solution.py:238
  36.1 0.0 collective-permute-done.3.recv_ref
  36.1 10.9 %shard_map.76 = (bf16[1024,128]{1,0:T(8,128)(2,1)}, f32[1024,128]{1,0:T(8,128)S(1)}, f32[1024,128]{1,0:T(8,128)S(1)}, bf16[16,256,128]{2,1,0:T(8,128)(2,1)}) custom-call(bf16[1024,128]{1,0:T(8,128)(2,1)S(1)} %bitcast.13, bf16[1024,128]{1,0:T(8,128)(2,1)S(1)} %collective-permute-done.q2_ref, bf16[1024,128]{1,0:T(8,128)(2,1)S(1)} %bitcast.16, ...), custom_call_target="tpu_custom_call" | custom-call | flops 5368709120 | bytes 5242880 | tf_op jit(solution)/shard_map/pallas_call | solution.py:215
  47.0 4.7 %all-to-all-start.1 = ((bf16[16,256,128]{2,1,0:T(8,128)(2,1)}), bf16[16,256,128]{2,1,0:T(8,128)(2,1)S(1)}, u32[]{:S(2)}, u32[]{:S(2)}) async-start(bf16[16,256,128]{2,1,0:T(8,128)(2,1)} %get-tuple-element.17), calls=%async_computation.1 | async-start | bytes 2097152 | tf_op jit(solution)/shard_map/all_to_all | solution.py:242
  51.7 0.1 collective-permute-start.4
  51.8 1.9 %collective-permute-done.4 = f32[1024,128]{1,0:T(8,128)S(1)} collective-permute-done((f32[1024,128]{1,0:T(8,128)S(1)}, f32[1024,128]{1,0:T(8,128)S(1)}, u32[]{:S(2)}, u32[]{:S(2)}) %collective-permute-start.4) | collective-permute-done | bytes 524320 | tf_op jit(solution)/shard_map/ppermute | solution.py:238
  53.7 0.8 %fusion = bf16[128,8,128]{2,1,0:T(8,128)(2,1)} fusion(f32[1024,128]{1,0:T(8,128)S(1)} %get-tuple-element.15, f32[1024,128]{1,0:T(8,128)S(1)} %collective-permute-done.4), kind=kLoop, calls=%fused_computation.1 | loop fusion | flops 262144 | bytes 1310720 | tf_op jit(solution)/shard_map/reshape | solution.py:259
  54.5 16.1 %all-to-all-done.1 = bf16[16,256,128]{2,1,0:T(8,128)(2,1)S(1)} async-done(((bf16[16,256,128]{2,1,0:T(8,128)(2,1)}), bf16[16,256,128]{2,1,0:T(8,128)(2,1)S(1)}, u32[]{:S(2)}, u32[]{:S(2)}) %all-to-all-start.1) | async-done | bytes 1048608 | tf_op jit(solution)/shard_map/all_to_all | solution.py:242
  70.6 0.1 reduce_sum.12
  70.8 0.6 slice_bitcast_fusion
Async XLA Ops:
  2.6 7.2 %copy-start = (bf16[128,8,128]{2,1,0:T(8,128)(2,1)S(1)}, bf16[128,8,128]{2,1,0:T(8,128)(2,1)}, u32[]{:S(2)}) copy-start(bf16[128,8,128]{2,1,0:T(8,128)(2,1)} %param.4) | copy-start | bytes 786436
  2.6 7.3 %copy-start.1 = (bf16[128,8,128]{2,1,0:T(8,128)(2,1)S(1)}, bf16[128,8,128]{2,1,0:T(8,128)(2,1)}, u32[]{:S(2)}) copy-start(bf16[128,8,128]{2,1,0:T(8,128)(2,1)} %param.7) | copy-start | bytes 786436
  2.6 25.4 %all-to-all-start = ((bf16[16,256,128]{2,1,0:T(8,128)(2,1)}), bf16[16,256,128]{2,1,0:T(8,128)(2,1)S(1)}, u32[]{:S(2)}, u32[]{:S(2)}) async-start(bf16[16,256,128]{2,1,0:T(8,128)(2,1)} %broadcast_in_dim.2), calls=%async_computation | async-start | bytes 2097152 | tf_op jit(solution)/shard_map/all_to_all | solution.py:242
  9.8 1.6 %collective-permute-start = (bf16[1024,128]{1,0:T(8,128)(2,1)S(1)}, bf16[1024,128]{1,0:T(8,128)(2,1)S(1)}, u32[]{:S(2)}, u32[]{:S(2)}) collective-permute-start(bf16[1024,128]{1,0:T(8,128)(2,1)S(1)} %bitcast.11), channel_id=1, source_target_pairs={{0,8},{8,0},{1,9},{9,1},{2,10},{10,2},{3,11},{11,3},{4,12},{12,4},... | collective-permute-start | bytes 786440 | tf_op jit(solution)/shard_map/ppermute | solution.py:238
  9.9 1.9 %collective-permute-start.1 = (bf16[1024,128]{1,0:T(8,128)(2,1)S(1)}, bf16[1024,128]{1,0:T(8,128)(2,1)S(1)}, u32[]{:S(2)}, u32[]{:S(2)}) collective-permute-start(bf16[1024,128]{1,0:T(8,128)(2,1)S(1)} %bitcast.14), channel_id=1, source_target_pairs={{0,8},{8,0},{1,9},{9,1},{2,10},{10,2},{3,11},{11,3},{4,12},{12,4},... | collective-permute-start | bytes 786440 | tf_op jit(solution)/shard_map/ppermute | solution.py:238
  34.3 1.7 %collective-permute-start.3 = (bf16[1024,128]{1,0:T(8,128)(2,1)S(1)}, bf16[1024,128]{1,0:T(8,128)(2,1)S(1)}, u32[]{:S(2)}, u32[]{:S(2)}) collective-permute-start(bf16[1024,128]{1,0:T(8,128)(2,1)S(1)} %get-tuple-element.13), channel_id=1, source_target_pairs={{0,8},{8,0},{1,9},{9,1},{2,10},{10,2},{3,11},{11,3},{4,12},{12,4},... | collective-permute-start | bytes 786440 | tf_op jit(solution)/shard_map/ppermute | solution.py:238
  34.4 1.6 %collective-permute-start.2 = (f32[8,2048]{1,0:T(8,128)S(1)}, f32[8,2048]{1,0:T(8,128)S(1)}, u32[]{:S(2)}, u32[]{:S(2)}) collective-permute-start(f32[8,2048]{1,0:T(8,128)S(1)} %get-tuple-element.11.stat_ref), channel_id=1, source_target_pairs={{0,8},{8,0},{1,9},{9,1},{2,10},{10,2},{3,11},{11,3},{4,12},{12,4},... | collective-permute-start | bytes 196616 | tf_op jit(solution)/shard_map/ppermute | solution.py:238
  47.0 23.6 %all-to-all-start.1 = ((bf16[16,256,128]{2,1,0:T(8,128)(2,1)}), bf16[16,256,128]{2,1,0:T(8,128)(2,1)S(1)}, u32[]{:S(2)}, u32[]{:S(2)}) async-start(bf16[16,256,128]{2,1,0:T(8,128)(2,1)} %get-tuple-element.17), calls=%async_computation.1 | async-start | bytes 2097152 | tf_op jit(solution)/shard_map/all_to_all | solution.py:242
  51.7 2.0 %collective-permute-start.4 = (f32[1024,128]{1,0:T(8,128)S(1)}, f32[1024,128]{1,0:T(8,128)S(1)}, u32[]{:S(2)}, u32[]{:S(2)}) collective-permute-start(f32[1024,128]{1,0:T(8,128)S(1)} %get-tuple-element.16), channel_id=1, source_target_pairs={{0,8},{8,0},{1,9},{9,1},{2,10},{10,2},{3,11},{11,3},{4,12},{12,4},... | collective-permute-start | bytes 1572872 | tf_op jit(solution)/shard_map/ppermute | solution.py:238

commit v4 on v3

--- a/solution.py
+++ b/solution.py
@@ -6,6 +6,7 @@
 from jax.experimental import pallas as pl
 from jax.experimental.pallas import tpu as pltpu
 from jax.sharding import Mesh, PartitionSpec as P
+
 
 HEAD_DIM = 128
 SCALE = HEAD_DIM ** (-0.5)
@@ -16,6 +17,7 @@
 ROWS = 128
 KEYS = NCHIP * ROWS
 QB = 256
+KF = 512
 KB = 512
 VMEM_LIMIT = 32 << 20
 F32 = jnp.float32
@@ -72,15 +74,23 @@
         peak = None
         for stage in range(rows // QB + 1):
             old_peak = peak
+            top = None
+            acc = None
+            for lo in range(0, KEYS, KF):
+                if stage < rows // QB:
+                    s = dot_t(k_all[lo:lo + KF, :], q_all[span(stage), :])
+                    s_bufs[stage % 2][lo:lo + KF, :] = s
+                    part = jnp.max(s.reshape(KF // 8, 8, QB), axis=0)
+                    top = part if top is None else jnp.maximum(top, part)
+                if stage > 0:
+                    b = stage - 1
+                    p = jnp.exp2(s_bufs[b % 2][lo:lo + KF, :] * EXP2_SCALE - old_peak).astype(BF16)
+                    term = dot(vt[:, lo:lo + KF], p)
+                    acc = term if acc is None else acc + term
             if stage < rows // QB:
-                s = dot_t(k_all[...], q_all[span(stage), :])
-                s_bufs[stage % 2][...] = s
-                top = jnp.max(s.reshape(KEYS // 8, 8, QB), axis=0)
                 peak = jnp.max(top, axis=0, keepdims=True) * EXP2_SCALE
             if stage > 0:
-                b = stage - 1
-                p = jnp.exp2(s_bufs[b % 2][...] * EXP2_SCALE - old_peak).astype(BF16)
-                finish(b, dot(vt[...], p), old_peak)
+                finish(stage - 1, acc, old_peak)
 
     pl.run_scoped(
         body,
@@ -242,17 +252,19 @@
     return lax.all_to_all(a, CHIPS, 0, 0, tiled=True)
 
 
-def on_device(queries, keys, values, out_grad):
+def step(queries, keys, values, out_grad):
     q = queries.reshape(-1, HEAD_DIM)
     g = out_grad.reshape(-1, HEAD_DIM)
     q2, g2 = swap_cores(q), swap_cores(g)
     kv = jnp.concatenate([keys[:, 0, :], values[:, 0, :]], axis=0)
-    kv = exchange(jnp.broadcast_to(kv[None], (NCHIP,) + kv.shape))
+    kv, q2, g2 = lax.optimization_barrier((jnp.broadcast_to(kv[None], (NCHIP,) + kv.shape), q2, g2))
+    kv = exchange(kv)
     stat, own, send = forward(q, q2, g, g2, kv)
     stat2, recv = swap_cores(stat), swap_cores(send)
     out, dq, dq_send, dkv = backward(q, q2, g, g2, kv, stat, stat2, own, recv)
+    dq_recv = swap_cores(dq_send)
     terms = exchange(dkv)
-    dq = (dq + swap_cores(dq_send)).astype(BF16)
+    dq = (dq + dq_recv).astype(BF16)
     total = jnp.sum(terms.astype(F32), axis=0).astype(BF16)
     return (
         out.reshape(queries.shape),
@@ -266,7 +278,7 @@
     fine = Mesh(mesh.devices.reshape(4, 2, 2, 2, 8), CHIPS + ("c", "z"))
     spec = P(CHIPS + ("c",), "z", None)
     return jax.shard_map(
-        on_device,
+        step,
         mesh=fine,
         in_specs=(spec,) * 4,
         out_specs=(spec,) * 4,

time: 72.1 us -> 70 us (0.971)
  blocking collectives: 0 us -> 24.3 us
  waiting for transfers between devices: 36.7 us -> 19.9 us
  starting transfers between devices: 13.2 us -> 5.19 us
  local copies, waits for them, and re-layouts: 1.81 us -> 0.84 us
    all_to_all x0 -> x1, blocking collectives: none -> 24.3 us  [exchange(): return lax.all_to_all(a, CHIPS, 0, 0, tiled=True)]
    all_to_all x2 -> x1, waiting for transfers between devices: 32.3 us -> 16.1 us  [exchange(): return lax.all_to_all(a, CHIPS, 0, 0, tiled=True)]
    all_to_all x2 -> x1, starting transfers between devices: 11.9 us -> 3.92 us  [exchange(): return lax.all_to_all(a, CHIPS, 0, 0, tiled=True)]
    broadcast_in_dim x1, local copies, waits for them, and re-layouts: 1.17 us -> 0.19 us  [step(): jnp.broadcast_to(kv[None], (NCHIP,) + kv.shape)]
    pallas_call x1, Pallas kernels: 6.38 us -> 5.65 us  [forward(): pl.pallas_call(forward_kernel, out_shape=(jax.ShapeDtypeStruct((8, 2 * n)...]
  transfers between devices with their start and end apart: 7 -> 6, of which waited for: 6 -> 5; matrix products, arithmetic and copies ran while one was open for 1% -> 2% of each run, Pallas kernels for 0% -> 0%
where the time goes in v4:
time: 70 us; the launch traced here: 69.3 us
  blocking collectives  24.3 us (35%)
  waiting for transfers between devices  19.9 us (28%)
  Pallas kernels  16.6 us (24%)
  starting transfers between devices  5.19 us (7%)
  other arithmetic  1.71 us (2%)
  local copies, waits for them, and re-layouts  0.84 us (1%)
    all_to_all x1, blocking collectives, exchange(): return lax.all_to_all(a, CHIPS, 0, 0, tiled=True)  24.3 us
    all_to_all x1, waiting for transfers between devices, exchange(): return lax.all_to_all(a, CHIPS, 0, 0, tiled=True)  16.1 us
    pallas_call x1, Pallas kernels, backward(): pl.pallas_call(backward_kernel, out_shape=(jax.ShapeDtypeStruct(q.shape,...  10.9 us
    pallas_call x1, Pallas kernels, forward(): pl.pallas_call(forward_kernel, out_shape=(jax.ShapeDtypeStruct((8, 2 * n)...  5.65 us
    all_to_all x1, starting transfers between devices, exchange(): return lax.all_to_all(a, CHIPS, 0, 0, tiled=True)  3.92 us
    ppermute x5, waiting for transfers between devices, swap_cores(): return lax.ppermute(a, 'c', [(0, 1), (1, 0)])  3.85 us
  transfers between devices with their start and end apart: 6, of which 5 were waited for; matrix products, arithmetic and copies ran while one was open for 2% of the time, Pallas kernels for 0%

profile of v4, /device:TPU:32, one launch (start us, length us, event | category | flops | bytes accessed | tf_op | source)
XLA Modules:
  0.0 69.3 jit_solution(10154786057129554421)
XLA Ops:
  0.6 0.1 collective-permute-start
  0.7 0.5 collective-permute-start.1
  1.2 0.8 %pad_maximum_fusion = bf16[256,128]{1,0:T(8,128)(2,1)S(1)} fusion(bf16[128,128]{1,0:T(8,128)(2,1)} %bitcast.17, bf16[128,128]{1,0:T(8,128)(2,1)} %bitcast.18), kind=kLoop, calls=%fused_computation.2 | loop fusion | flops 131072 | bytes 131072 | tf_op jit(solution)/shard_map/concatenate | solution.py:259
  2.0 0.5 collective-permute-done.q2_ref
  2.5 0.4 collective-permute-done.1.g2_ref
  2.8 0.2 broadcast_in_dim.2
  3.0 0.0 copy-start
  3.1 0.0 copy-start.1
  3.1 24.3 %all_to_all.10.kv_ref = bf16[16,256,128]{2,1,0:T(8,128)(2,1)S(1)} all-to-all(bf16[16,256,128]{2,1,0:T(8,128)(2,1)S(1)} %broadcast_in_dim.2), channel_id=1, replica_groups=mesh['x'=4,'yl'=2,'yh'=2,'c'=2,'z'=8] {'x','yl','yh'}, dimensions={0} | all-to-all | bytes 2097152 | tf_op jit(solution)/shard_map/all_to_all | solution.py:252
  27.4 0.0 copy-done
  27.4 0.0 copy-done.1
  27.4 5.6 %shard_map.75 = (f32[8,2048]{1,0:T(8,128)S(1)}, f32[1024,128]{1,0:T(8,128)S(1)}, bf16[1024,128]{1,0:T(8,128)(2,1)S(1)}) custom-call(bf16[1024,128]{1,0:T(8,128)(2,1)S(1)} %bitcast.12, bf16[1024,128]{1,0:T(8,128)(2,1)S(1)} %collective-permute-done.q2_ref, bf16[1024,128]{1,0:T(8,128)(2,1)S(1)} %bitcast.15, ...), custom_call_target="tpu_custom_call" | custom-call | flops 2147483648 | bytes 3145728 | tf_op jit(solution)/shard_map/pallas_call | solution.py:205
  33.0 0.1 collective-permute-start.3
  33.1 0.5 collective-permute-start.2
  33.6 1.1 %collective-permute-done.2.stat2_ref = f32[8,2048]{1,0:T(8,128)S(1)} collective-permute-done((f32[8,2048]{1,0:T(8,128)S(1)}, f32[8,2048]{1,0:T(8,128)S(1)}, u32[]{:S(2)}, u32[]{:S(2)}) %collective-permute-start.2) | collective-permute-done | bytes 65568 | tf_op jit(solution)/shard_map/ppermute | solution.py:248
  34.8 0.0 collective-permute-done.3.recv_ref
  34.8 10.9 %shard_map.76 = (bf16[1024,128]{1,0:T(8,128)(2,1)}, f32[1024,128]{1,0:T(8,128)S(1)}, f32[1024,128]{1,0:T(8,128)S(1)}, bf16[16,256,128]{2,1,0:T(8,128)(2,1)}) custom-call(bf16[1024,128]{1,0:T(8,128)(2,1)S(1)} %bitcast.13, bf16[1024,128]{1,0:T(8,128)(2,1)S(1)} %collective-permute-done.q2_ref, bf16[1024,128]{1,0:T(8,128)(2,1)S(1)} %bitcast.16, ...), custom_call_target="tpu_custom_call" | custom-call | flops 5368709120 | bytes 5242880 | tf_op jit(solution)/shard_map/pallas_call | solution.py:225
  45.7 3.9 %all-to-all-start.1 = ((bf16[16,256,128]{2,1,0:T(8,128)(2,1)}), bf16[16,256,128]{2,1,0:T(8,128)(2,1)S(1)}, u32[]{:S(2)}, u32[]{:S(2)}) async-start(bf16[16,256,128]{2,1,0:T(8,128)(2,1)} %get-tuple-element.23), calls=%async_computation.1 | async-start | bytes 2097152 | tf_op jit(solution)/shard_map/all_to_all | solution.py:252
  49.6 0.1 collective-permute-start.4
  49.7 1.9 %collective-permute-done.4 = f32[1024,128]{1,0:T(8,128)S(1)} collective-permute-done((f32[1024,128]{1,0:T(8,128)S(1)}, f32[1024,128]{1,0:T(8,128)S(1)}, u32[]{:S(2)}, u32[]{:S(2)}) %collective-permute-start.4) | collective-permute-done | bytes 524320 | tf_op jit(solution)/shard_map/ppermute | solution.py:248
  51.6 0.8 %fusion = bf16[128,8,128]{2,1,0:T(8,128)(2,1)} fusion(f32[1024,128]{1,0:T(8,128)S(1)} %get-tuple-element.21, f32[1024,128]{1,0:T(8,128)S(1)} %collective-permute-done.4), kind=kLoop, calls=%fused_computation.1 | loop fusion | flops 262144 | bytes 1310720 | tf_op jit(solution)/shard_map/reshape | solution.py:271
  52.4 16.1 %all-to-all-done.1 = bf16[16,256,128]{2,1,0:T(8,128)(2,1)S(1)} async-done(((bf16[16,256,128]{2,1,0:T(8,128)(2,1)}), bf16[16,256,128]{2,1,0:T(8,128)(2,1)S(1)}, u32[]{:S(2)}, u32[]{:S(2)}) %all-to-all-start.1) | async-done | bytes 1048608 | tf_op jit(solution)/shard_map/all_to_all | solution.py:252
  68.5 0.1 reduce_sum.12
  68.6 0.6 slice_bitcast_fusion
Async XLA Ops:
  0.6 1.8 %collective-permute-start = (bf16[1024,128]{1,0:T(8,128)(2,1)}, bf16[1024,128]{1,0:T(8,128)(2,1)S(1)}, u32[]{:S(2)}, u32[]{:S(2)}) collective-permute-start(bf16[1024,128]{1,0:T(8,128)(2,1)} %bitcast.11), channel_id=1, source_target_pairs={{0,8},{8,0},{1,9},{9,1},{2,10},{10,2},{3,11},{11,3},{4,12},{12,4},... | collective-permute-start | bytes 786440 | tf_op jit(solution)/shard_map/ppermute | solution.py:248
  0.7 2.1 %collective-permute-start.1 = (bf16[1024,128]{1,0:T(8,128)(2,1)}, bf16[1024,128]{1,0:T(8,128)(2,1)S(1)}, u32[]{:S(2)}, u32[]{:S(2)}) collective-permute-start(bf16[1024,128]{1,0:T(8,128)(2,1)} %bitcast.14), channel_id=1, source_target_pairs={{0,8},{8,0},{1,9},{9,1},{2,10},{10,2},{3,11},{11,3},{4,12},{12,4},... | collective-permute-start | bytes 786440 | tf_op jit(solution)/shard_map/ppermute | solution.py:248
  3.0 24.3 %copy-start = (bf16[128,8,128]{2,1,0:T(8,128)(2,1)S(1)}, bf16[128,8,128]{2,1,0:T(8,128)(2,1)}, u32[]{:S(2)}) copy-start(bf16[128,8,128]{2,1,0:T(8,128)(2,1)} %param.4) | copy-start | bytes 786436
  3.1 24.3 %copy-start.1 = (bf16[128,8,128]{2,1,0:T(8,128)(2,1)S(1)}, bf16[128,8,128]{2,1,0:T(8,128)(2,1)}, u32[]{:S(2)}) copy-start(bf16[128,8,128]{2,1,0:T(8,128)(2,1)} %param.7) | copy-start | bytes 786436
  33.0 1.7 %collective-permute-start.3 = (bf16[1024,128]{1,0:T(8,128)(2,1)S(1)}, bf16[1024,128]{1,0:T(8,128)(2,1)S(1)}, u32[]{:S(2)}, u32[]{:S(2)}) collective-permute-start(bf16[1024,128]{1,0:T(8,128)(2,1)S(1)} %get-tuple-element.19), channel_id=1, source_target_pairs={{0,8},{8,0},{1,9},{9,1},{2,10},{10,2},{3,11},{11,3},{4,12},{12,4},... | collective-permute-start | bytes 786440 | tf_op jit(solution)/shard_map/ppermute | solution.py:248
  33.1 1.6 %collective-permute-start.2 = (f32[8,2048]{1,0:T(8,128)S(1)}, f32[8,2048]{1,0:T(8,128)S(1)}, u32[]{:S(2)}, u32[]{:S(2)}) collective-permute-start(f32[8,2048]{1,0:T(8,128)S(1)} %get-tuple-element.17.stat_ref), channel_id=1, source_target_pairs={{0,8},{8,0},{1,9},{9,1},{2,10},{10,2},{3,11},{11,3},{4,12},{12,4},... | collective-permute-start | bytes 196616 | tf_op jit(solution)/shard_map/ppermute | solution.py:248
  45.7 22.8 %all-to-all-start.1 = ((bf16[16,256,128]{2,1,0:T(8,128)(2,1)}), bf16[16,256,128]{2,1,0:T(8,128)(2,1)S(1)}, u32[]{:S(2)}, u32[]{:S(2)}) async-start(bf16[16,256,128]{2,1,0:T(8,128)(2,1)} %get-tuple-element.23), calls=%async_computation.1 | async-start | bytes 2097152 | tf_op jit(solution)/shard_map/all_to_all | solution.py:252
  49.6 2.0 %collective-permute-start.4 = (f32[1024,128]{1,0:T(8,128)S(1)}, f32[1024,128]{1,0:T(8,128)S(1)}, u32[]{:S(2)}, u32[]{:S(2)}) collective-permute-start(f32[1024,128]{1,0:T(8,128)S(1)} %get-tuple-element.22), channel_id=1, source_target_pairs={{0,8},{8,0},{1,9},{9,1},{2,10},{10,2},{3,11},{11,3},{4,12},{12,4},... | collective-permute-start | bytes 1572872 | tf_op jit(solution)/shard_map/ppermute | solution.py:248

commit v5 on v4

--- a/solution.py
+++ b/solution.py
@@ -36,11 +36,7 @@
     return slice(b * QB, (b + 1) * QB)
 
 
-def as_rows(line):
-    return jnp.transpose(jnp.broadcast_to(line, (HEAD_DIM, line.shape[1])))
-
-
-def forward_kernel(q_ref, q2_ref, g_ref, g2_ref, kv_ref, stat_ref, own_ref, send_ref, s0, s1):
+def forward_kernel(q_ref, q2_ref, g_ref, g2_ref, kv_ref, stat_ref, half_ref, s0, s1):
     own_rows = q_ref.shape[0]
     rows = 2 * own_rows
 
@@ -64,11 +60,7 @@
             stat_ref[0:1, qs] = peak
             stat_ref[1:2, qs] = total
             stat_ref[2:3, qs] = jnp.sum(grad_t * out_t, axis=0, keepdims=True)
-            out = jnp.transpose(out_t)
-            if half == 0:
-                own_ref[local, :] = out
-            else:
-                send_ref[local, :] = out.astype(BF16)
+            half_ref[:, qs] = out_t
 
         s_bufs = (s0, s1)
         peak = None
@@ -101,8 +93,8 @@
 
 
 def backward_kernel(
-    q_ref, q2_ref, g_ref, g2_ref, kv_ref, stat_ref, stat2_ref, own_ref, recv_ref,
-    out_ref, dq_ref, send_ref, dkv_ref,
+    q_ref, q2_ref, g_ref, g2_ref, kv_ref, stat_ref, stat2_ref, half_ref,
+    keep_ref, send_ref, dkv_ref,
     lse, dots, dqt,
 ):
     own_rows = q_ref.shape[0]
@@ -131,18 +123,16 @@
             total_a = stat_ref[1:2, here] * jnp.exp2(peak_a - peak)
             total_b = stat2_ref[1:2, there] * jnp.exp2(peak_b - peak)
             total = total_a + total_b
-            weight_a, weight_b = total_a / total, total_b / total
+            weight_a = total_a / total
             lse[:, here] = jnp.broadcast_to(peak + jnp.log(total) * LOG2E, (8, own_rows))
             dots[:, here] = jnp.broadcast_to(
-                weight_a * stat_ref[2:3, here] + weight_b * stat2_ref[2:3, there], (8, own_rows)
+                weight_a * stat_ref[2:3, here] + total_b / total * stat2_ref[2:3, there], (8, own_rows)
             )
-            if half == 0:
-                for lo in range(0, own_rows, QB):
-                    local = slice(lo, lo + QB)
-                    out_ref[local, :] = (
-                        own_ref[local, :] * as_rows(weight_a[:, local])
-                        + recv_ref[local, :].astype(F32) * as_rows(weight_b[:, local])
-                    ).astype(BF16)
+            for lo in range(0, own_rows, QB):
+                at = half * own_rows + lo
+                (keep_ref, send_ref)[half][lo:lo + QB, :] = jnp.transpose(
+                    half_ref[:, at:at + QB] * weight_a[:, lo:lo + QB]
+                )
 
         dqt[...] = jnp.zeros_like(dqt)
         p_bufs, ds_bufs = (p0, p1), (ds0, ds1)
@@ -186,7 +176,8 @@
                         query_grad(prior, 2 * b - 7)
         for b in range(nq):
             half, lo = divmod(b * QB, own_rows)
-            (dq_ref, send_ref)[half][lo:lo + QB, :] = jnp.transpose(dqt[:, span(b)]) * SCALE
+            at = own_rows + lo
+            (keep_ref, send_ref)[half][at:at + QB, :] = jnp.transpose(dqt[:, span(b)]) * SCALE
 
     pl.run_scoped(
         body,
@@ -206,11 +197,10 @@
         forward_kernel,
         out_shape=(
             jax.ShapeDtypeStruct((8, 2 * n), F32),
-            jax.ShapeDtypeStruct(q.shape, F32),
-            jax.ShapeDtypeStruct(q.shape, BF16),
+            jax.ShapeDtypeStruct((HEAD_DIM, 2 * n), F32),
         ),
         in_specs=[vmem] * 5,
-        out_specs=(vmem,) * 3,
+        out_specs=(vmem,) * 2,
         scratch_shapes=[pltpu.VMEM((KEYS, QB), F32), pltpu.VMEM((KEYS, QB), F32)],
         cost_estimate=pl.CostEstimate(
             flops=8 * n * KEYS * HEAD_DIM, transcendentals=2 * n * KEYS, bytes_accessed=3 << 20
@@ -219,19 +209,18 @@
     )(q, q2, g, g2, kv)
 
 
-def backward(q, q2, g, g2, kv, stat, stat2, own, recv):
+def backward(q, q2, g, g2, kv, stat, stat2, half):
     n = q.shape[0]
     vmem = pl.BlockSpec(memory_space=pltpu.VMEM)
     return pl.pallas_call(
         backward_kernel,
         out_shape=(
-            jax.ShapeDtypeStruct(q.shape, BF16),
-            jax.ShapeDtypeStruct(q.shape, F32),
-            jax.ShapeDtypeStruct(q.shape, F32),
+            jax.ShapeDtypeStruct((2 * n, HEAD_DIM), F32),
+            jax.ShapeDtypeStruct((2 * n, HEAD_DIM), F32),
             jax.ShapeDtypeStruct(kv.shape, BF16),
         ),
-        in_specs=[vmem] * 9,
-        out_specs=(vmem,) * 4,
+        in_specs=[vmem] * 8,
+        out_specs=(vmem,) * 3,
         scratch_shapes=[
             pltpu.VMEM((8, 2 * n), F32),
             pltpu.VMEM((8, 2 * n), F32),
@@ -241,7 +230,27 @@
             flops=20 * n * KEYS * HEAD_DIM, transcendentals=2 * n * KEYS, bytes_accessed=5 << 20
         ),
         compiler_params=pltpu.CompilerParams(vmem_limit_bytes=VMEM_LIMIT),
-    )(q, q2, g, g2, kv, stat, stat2, own, recv)
+    )(q, q2, g, g2, kv, stat, stat2, half)
+
+
+def join_kernel(keep_ref, recv_ref, total_ref, out_ref, dq_ref, dk_ref, dv_ref):
+    n = out_ref.shape[0]
+    out_ref[...] = (keep_ref[:n, :] + recv_ref[:n, :]).astype(BF16)
+    dq_ref[...] = (keep_ref[n:, :] + recv_ref[n:, :]).astype(BF16)
+    dk_ref[...] = total_ref[:ROWS, :]
+    dv_ref[...] = total_ref[ROWS:, :]
+
+
+def join(keep, recv, total):
+    n = keep.shape[0] // 2
+    vmem = pl.BlockSpec(memory_space=pltpu.VMEM)
+    return pl.pallas_call(
+        join_kernel,
+        out_shape=tuple(jax.ShapeDtypeStruct((m, HEAD_DIM), BF16) for m in (n, n, ROWS, ROWS)),
+        in_specs=[vmem] * 3,
+        out_specs=(vmem,) * 4,
+        compiler_params=pltpu.CompilerParams(vmem_limit_bytes=8 << 20),
+    )(keep, recv, total)
 
 
 def swap_cores(a):
@@ -259,18 +268,17 @@
     kv = jnp.concatenate([keys[:, 0, :], values[:, 0, :]], axis=0)
     kv, q2, g2 = lax.optimization_barrier((jnp.broadcast_to(kv[None], (NCHIP,) + kv.shape), q2, g2))
     kv = exchange(kv)
-    stat, own, send = forward(q, q2, g, g2, kv)
-    stat2, recv = swap_cores(stat), swap_cores(send)
-    out, dq, dq_send, dkv = backward(q, q2, g, g2, kv, stat, stat2, own, recv)
-    dq_recv = swap_cores(dq_send)
+    stat, half = forward(q, q2, g, g2, kv)
+    keep, send, dkv = backward(q, q2, g, g2, kv, stat, swap_cores(stat), half)
+    recv = swap_cores(send)
     terms = exchange(dkv)
-    dq = (dq + dq_recv).astype(BF16)
     total = jnp.sum(terms.astype(F32), axis=0).astype(BF16)
+    out, dq, dk, dv = join(keep, recv, total)
     return (
         out.reshape(queries.shape),
         dq.reshape(queries.shape),
-        total[:ROWS].reshape(keys.shape),
-        total[ROWS:].reshape(values.shape),
+        dk.reshape(keys.shape),
+        dv.reshape(values.shape),
     )
 
 

time: 70 us -> 69 us (0.986)
  blocking collectives: 24.3 us -> 45.7 us
  waiting for transfers between devices: 19.9 us -> 2.07 us
  starting transfers between devices: 5.19 us -> 1.11 us
    all_to_all x1 -> x2, blocking collectives: 24.3 us -> 45.7 us  [exchange(): return lax.all_to_all(a, CHIPS, 0, 0, tiled=True)]
    all_to_all x1 -> x0, waiting for transfers between devices: 16.1 us -> none  [exchange(): return lax.all_to_all(a, CHIPS, 0, 0, tiled=True)]
    all_to_all x1 -> x0, starting transfers between devices: 3.92 us -> none  [exchange(): return lax.all_to_all(a, CHIPS, 0, 0, tiled=True)]
    ppermute x5 -> x4, waiting for transfers between devices: 3.85 us -> 2.07 us  [swap_cores(): return lax.ppermute(a, 'c', [(0, 1), (1, 0)])]
    reduce_sum x1, other arithmetic: 0.14 us -> 1.37 us  [step(): total = jnp.sum(terms.astype(F32), axis=0).astype(BF16)]
    reshape x1 -> x0, other arithmetic: 0.78 us -> none  [step(): dq.reshape(queries.shape)]
    pallas_call x1 -> x2, Pallas kernels: 10.9 us -> 11.1 us  [the longest x1 10.2 us: backward(): pl.pallas_call(backward_kernel, out_shape=(jax.ShapeDtypeStruct((2 * n, H...]
  transfers between devices with their start and end apart: 6 -> 4, of which waited for: 5 -> 3; matrix products, arithmetic and copies ran while one was open for 2% -> 3% of each run, Pallas kernels for 0% -> 0%
where the time goes in v5:
time: 69 us; the launch traced here: 68.7 us
  blocking collectives  45.7 us (66%)
  Pallas kernels  16.8 us (24%)
  other arithmetic  2.15 us (3%)
  waiting for transfers between devices  2.07 us (3%)
  starting transfers between devices  1.11 us (2%)
  between operations  0.7 us (1%)
    all_to_all x2, blocking collectives, exchange(): return lax.all_to_all(a, CHIPS, 0, 0, tiled=True)  45.7 us
    pallas_call x1, Pallas kernels, backward(): pl.pallas_call(backward_kernel, out_shape=(jax.ShapeDtypeStruct((2 * n, H...  10.2 us
    pallas_call x1, Pallas kernels, forward(): pl.pallas_call(forward_kernel, out_shape=(jax.ShapeDtypeStruct((8, 2 * n)...  5.66 us
    ppermute x4, waiting for transfers between devices, swap_cores(): return lax.ppermute(a, 'c', [(0, 1), (1, 0)])  2.07 us
  transfers between devices with their start and end apart: 4, of which 3 were waited for; matrix products, arithmetic and copies ran while one was open for 3% of the time, Pallas kernels for 0%

profile of v5, /device:TPU:32, one launch (start us, length us, event | category | flops | bytes accessed | tf_op | source)
XLA Modules:
  0.0 68.7 jit_solution(9599804879070169096)
XLA Ops:
  0.6 0.1 collective-permute-start
  0.7 0.5 collective-permute-start.1
  1.2 0.8 %pad_maximum_fusion = bf16[256,128]{1,0:T(8,128)(2,1)S(1)} fusion(bf16[128,128]{1,0:T(8,128)(2,1)} %bitcast.14, bf16[128,128]{1,0:T(8,128)(2,1)} %bitcast.15), kind=kLoop, calls=%fused_computation | loop fusion | flops 131072 | bytes 131072 | tf_op jit(solution)/shard_map/concatenate | solution.py:268
  2.0 0.5 collective-permute-done.q2_ref
  2.5 0.4 collective-permute-done.1.g2_ref
  2.8 0.2 broadcast_in_dim.2
  3.0 0.0 copy-start
  3.1 0.0 copy-start.1
  3.1 24.3 %all_to_all.10.kv_ref = bf16[16,256,128]{2,1,0:T(8,128)(2,1)S(1)} all-to-all(bf16[16,256,128]{2,1,0:T(8,128)(2,1)S(1)} %broadcast_in_dim.2), channel_id=1, replica_groups=mesh['x'=4,'yl'=2,'yh'=2,'c'=2,'z'=8] {'x','yl','yh'}, dimensions={0} | all-to-all | bytes 2097152 | tf_op jit(solution)/shard_map/all_to_all | solution.py:261
  27.4 0.0 copy-done
  27.4 0.0 copy-done.1
  27.4 5.7 %shard_map.75 = (f32[8,2048]{1,0:T(8,128)S(1)}, f32[128,2048]{1,0:T(8,128)S(1)}) custom-call(bf16[1024,128]{1,0:T(8,128)(2,1)S(1)} %bitcast.9, bf16[1024,128]{1,0:T(8,128)(2,1)S(1)} %collective-permute-done.q2_ref, bf16[1024,128]{1,0:T(8,128)(2,1)S(1)} %bitcast.12, bf16[1024,128]{1,0:T(8,128)(2,1)S(1)} %collective-permute-done.1.g2_ref, ...), custom_call_target="tpu_custom_call" | custom-call | flops 2147483648 | bytes 3145728 | tf_op jit(solution)/shard_map/pallas_call | solution.py:196
  33.1 0.3 collective-permute-start.2
  33.3 1.2 %collective-permute-done.2.stat2_ref = f32[8,2048]{1,0:T(8,128)S(1)} collective-permute-done((f32[8,2048]{1,0:T(8,128)S(1)}, f32[8,2048]{1,0:T(8,128)S(1)}, u32[]{:S(2)}, u32[]{:S(2)}) %collective-permute-start.2) | collective-permute-done | bytes 65568 | tf_op jit(solution)/shard_map/ppermute | solution.py:257
  34.6 10.2 %shard_map.76 = (f32[2048,128]{1,0:T(8,128)S(1)}, f32[2048,128]{1,0:T(8,128)S(1)}, bf16[16,256,128]{2,1,0:T(8,128)(2,1)S(1)}) custom-call(bf16[1024,128]{1,0:T(8,128)(2,1)S(1)} %bitcast.10, bf16[1024,128]{1,0:T(8,128)(2,1)S(1)} %collective-permute-done.q2_ref, bf16[1024,128]{1,0:T(8,128)(2,1)S(1)} %bitcast.13, ...), custom_call_target="tpu_custom_call" | custom-call | flops 5368709120 | bytes 5242880 | tf_op jit(solution)/shard_map/pallas_call | solution.py:215
  44.8 0.2 collective-permute-start.3
  45.0 21.4 %all_to_all.11 = bf16[16,256,128]{2,1,0:T(8,128)(2,1)} all-to-all(bf16[16,256,128]{2,1,0:T(8,128)(2,1)S(1)} %get-tuple-element.23), channel_id=1, replica_groups=mesh['x'=4,'yl'=2,'yh'=2,'c'=2,'z'=8] {'x','yl','yh'}, dimensions={0} | all-to-all | bytes 2097152 | tf_op jit(solution)/shard_map/all_to_all | solution.py:261
  66.4 1.4 %reduce_sum.12.total_ref = bf16[256,128]{1,0:T(8,128)(2,1)S(1)} reduce(bf16[16,256,128]{2,1,0:T(8,128)(2,1)} %all_to_all.11, bf16[]{:T(256)} %constant.2.clone.1), dimensions={0}, to_apply=%region_0.0 | reduce | flops 491520 | bytes 1114114 | tf_op jit(solution)/shard_map/reduce_sum | solution.py:275
  67.8 0.0 collective-permute-done.3.recv_ref
  67.8 0.9 %shard_map.77 = (bf16[1024,128]{1,0:T(8,128)(2,1)}, bf16[1024,128]{1,0:T(8,128)(2,1)}, bf16[128,128]{1,0:T(8,128)(2,1)}, bf16[128,128]{1,0:T(8,128)(2,1)}) custom-call(f32[2048,128]{1,0:T(8,128)S(1)} %get-tuple-element.21.keep_ref, f32[2048,128]{1,0:T(8,128)S(1)} %collective-permute-done.3.recv_ref, bf16[256,128]{1,0:T(8,128)(2,1)S(1)} %reduce_sum.12.total_ref), custom_call_target="tpu_custom_call" | custom-call | tf_op jit(solution)/shard_map/pallas_call | solution.py:247
Async XLA Ops:
  0.6 1.8 %collective-permute-start = (bf16[1024,128]{1,0:T(8,128)(2,1)}, bf16[1024,128]{1,0:T(8,128)(2,1)S(1)}, u32[]{:S(2)}, u32[]{:S(2)}) collective-permute-start(bf16[1024,128]{1,0:T(8,128)(2,1)} %bitcast.8), channel_id=1, source_target_pairs={{0,8},{8,0},{1,9},{9,1},{2,10},{10,2},{3,11},{11,3},{4,12},{12,4},... | collective-permute-start | bytes 786440 | tf_op jit(solution)/shard_map/ppermute | solution.py:257
  0.7 2.1 %collective-permute-start.1 = (bf16[1024,128]{1,0:T(8,128)(2,1)}, bf16[1024,128]{1,0:T(8,128)(2,1)S(1)}, u32[]{:S(2)}, u32[]{:S(2)}) collective-permute-start(bf16[1024,128]{1,0:T(8,128)(2,1)} %bitcast.11), channel_id=1, source_target_pairs={{0,8},{8,0},{1,9},{9,1},{2,10},{10,2},{3,11},{11,3},{4,12},{12,4},... | collective-permute-start | bytes 786440 | tf_op jit(solution)/shard_map/ppermute | solution.py:257
  3.0 24.3 %copy-start = (bf16[128,8,128]{2,1,0:T(8,128)(2,1)S(1)}, bf16[128,8,128]{2,1,0:T(8,128)(2,1)}, u32[]{:S(2)}) copy-start(bf16[128,8,128]{2,1,0:T(8,128)(2,1)} %param.4) | copy-start | bytes 786436
  3.1 24.3 %copy-start.1 = (bf16[128,8,128]{2,1,0:T(8,128)(2,1)S(1)}, bf16[128,8,128]{2,1,0:T(8,128)(2,1)}, u32[]{:S(2)}) copy-start(bf16[128,8,128]{2,1,0:T(8,128)(2,1)} %param.7) | copy-start | bytes 786436
  33.1 1.5 %collective-permute-start.2 = (f32[8,2048]{1,0:T(8,128)S(1)}, f32[8,2048]{1,0:T(8,128)S(1)}, u32[]{:S(2)}, u32[]{:S(2)}) collective-permute-start(f32[8,2048]{1,0:T(8,128)S(1)} %get-tuple-element.19.stat_ref), channel_id=1, source_target_pairs={{0,8},{8,0},{1,9},{9,1},{2,10},{10,2},{3,11},{11,3},{4,12},{12,4},... | collective-permute-start | bytes 196616 | tf_op jit(solution)/shard_map/ppermute | solution.py:257
  44.8 23.0 %collective-permute-start.3 = (f32[2048,128]{1,0:T(8,128)S(1)}, f32[2048,128]{1,0:T(8,128)S(1)}, u32[]{:S(2)}, u32[]{:S(2)}) collective-permute-start(f32[2048,128]{1,0:T(8,128)S(1)} %get-tuple-element.22), channel_id=1, source_target_pairs={{0,8},{8,0},{1,9},{9,1},{2,10},{10,2},{3,11},{11,3},{4,12},{12,4},... | collective-permute-start | bytes 3145736 | tf_op jit(solution)/shard_map/ppermute | solution.py:257

commit v6 on v5

--- a/solution.py
+++ b/solution.py
@@ -233,12 +233,13 @@
     )(q, q2, g, g2, kv, stat, stat2, half)
 
 
-def join_kernel(keep_ref, recv_ref, total_ref, out_ref, dq_ref, dk_ref, dv_ref):
+def join_kernel(keep_ref, recv_ref, terms_ref, out_ref, dq_ref, dk_ref, dv_ref):
     n = out_ref.shape[0]
     out_ref[...] = (keep_ref[:n, :] + recv_ref[:n, :]).astype(BF16)
     dq_ref[...] = (keep_ref[n:, :] + recv_ref[n:, :]).astype(BF16)
-    dk_ref[...] = total_ref[:ROWS, :]
-    dv_ref[...] = total_ref[ROWS:, :]
+    total = jnp.sum(terms_ref[...].astype(F32), axis=0).astype(BF16)
+    dk_ref[...] = total[:ROWS, :]
+    dv_ref[...] = total[ROWS:, :]
 
 
 def join(keep, recv, total):
@@ -272,8 +273,7 @@
     keep, send, dkv = backward(q, q2, g, g2, kv, stat, swap_cores(stat), half)
     recv = swap_cores(send)
     terms = exchange(dkv)
-    total = jnp.sum(terms.astype(F32), axis=0).astype(BF16)
-    out, dq, dk, dv = join(keep, recv, total)
+    out, dq, dk, dv = join(keep, recv, terms)
     return (
         out.reshape(queries.shape),
         dq.reshape(queries.shape),

time: 69 us -> 67.5 us (0.978)
  other arithmetic: 2.15 us -> 0.78 us
    reduce_sum x1 -> x0, other arithmetic: 1.37 us -> none  [step(): total = jnp.sum(terms.astype(F32), axis=0).astype(BF16)]
  transfers between devices with their start and end apart: 4 -> 4, of which waited for: 3 -> 3; matrix products, arithmetic and copies ran while one was open for 3% -> 1% of each run, Pallas kernels for 0% -> 0%
where the time goes in v6:
time: 67.5 us; the launch traced here: 67.2 us
  blocking collectives  45.6 us (68%)
  Pallas kernels  16.8 us (25%)
  waiting for transfers between devices  2.07 us (3%)
  starting transfers between devices  1.11 us (2%)
  other arithmetic  0.78 us (1%)
  between operations  0.69 us (1%)
    all_to_all x2, blocking collectives, exchange(): return lax.all_to_all(a, CHIPS, 0, 0, tiled=True)  45.6 us
    pallas_call x1, Pallas kernels, backward(): pl.pallas_call(backward_kernel, out_shape=(jax.ShapeDtypeStruct((2 * n, H...  10.2 us
    pallas_call x1, Pallas kernels, forward(): pl.pallas_call(forward_kernel, out_shape=(jax.ShapeDtypeStruct((8, 2 * n)...  5.66 us
    ppermute x4, waiting for transfers between devices, swap_cores(): return lax.ppermute(a, 'c', [(0, 1), (1, 0)])  2.07 us
  transfers between devices with their start and end apart: 4, of which 3 were waited for; matrix products, arithmetic and copies ran while one was open for 1% of the time, Pallas kernels for 0%

profile of v6, /device:TPU:32, one launch (start us, length us, event | category | flops | bytes accessed | tf_op | source)
XLA Modules:
  0.0 67.2 jit_solution(9722862735778881313)
XLA Ops:
  0.6 0.1 collective-permute-start
  0.7 0.5 collective-permute-start.1
  1.2 0.8 %pad_maximum_fusion = bf16[256,128]{1,0:T(8,128)(2,1)S(1)} fusion(bf16[128,128]{1,0:T(8,128)(2,1)} %bitcast.14, bf16[128,128]{1,0:T(8,128)(2,1)} %bitcast.15), kind=kLoop, calls=%fused_computation | loop fusion | flops 131072 | bytes 131072 | tf_op jit(solution)/shard_map/concatenate | solution.py:269
  2.0 0.5 collective-permute-done.q2_ref
  2.5 0.4 collective-permute-done.1.g2_ref
  2.8 0.2 broadcast_in_dim.2
  3.0 0.0 copy-start
  3.1 0.0 copy-start.1
  3.1 24.3 %all_to_all.10.kv_ref = bf16[16,256,128]{2,1,0:T(8,128)(2,1)S(1)} all-to-all(bf16[16,256,128]{2,1,0:T(8,128)(2,1)S(1)} %broadcast_in_dim.2), channel_id=1, replica_groups=mesh['x'=4,'yl'=2,'yh'=2,'c'=2,'z'=8] {'x','yl','yh'}, dimensions={0} | all-to-all | bytes 2097152 | tf_op jit(solution)/shard_map/all_to_all | solution.py:262
  27.4 0.0 copy-done
  27.4 0.0 copy-done.1
  27.4 5.7 %shard_map.75 = (f32[8,2048]{1,0:T(8,128)S(1)}, f32[128,2048]{1,0:T(8,128)S(1)}) custom-call(bf16[1024,128]{1,0:T(8,128)(2,1)S(1)} %bitcast.9, bf16[1024,128]{1,0:T(8,128)(2,1)S(1)} %collective-permute-done.q2_ref, bf16[1024,128]{1,0:T(8,128)(2,1)S(1)} %bitcast.12, bf16[1024,128]{1,0:T(8,128)(2,1)S(1)} %collective-permute-done.1.g2_ref, ...), custom_call_target="tpu_custom_call" | custom-call | flops 2147483648 | bytes 3145728 | tf_op jit(solution)/shard_map/pallas_call | solution.py:196
  33.1 0.3 collective-permute-start.2
  33.3 1.2 %collective-permute-done.2.stat2_ref = f32[8,2048]{1,0:T(8,128)S(1)} collective-permute-done((f32[8,2048]{1,0:T(8,128)S(1)}, f32[8,2048]{1,0:T(8,128)S(1)}, u32[]{:S(2)}, u32[]{:S(2)}) %collective-permute-start.2) | collective-permute-done | bytes 65568 | tf_op jit(solution)/shard_map/ppermute | solution.py:258
  34.6 10.2 %shard_map.76 = (f32[2048,128]{1,0:T(8,128)S(1)}, f32[2048,128]{1,0:T(8,128)S(1)}, bf16[16,256,128]{2,1,0:T(8,128)(2,1)S(1)}) custom-call(bf16[1024,128]{1,0:T(8,128)(2,1)S(1)} %bitcast.10, bf16[1024,128]{1,0:T(8,128)(2,1)S(1)} %collective-permute-done.q2_ref, bf16[1024,128]{1,0:T(8,128)(2,1)S(1)} %bitcast.13, ...), custom_call_target="tpu_custom_call" | custom-call | flops 5368709120 | bytes 5242880 | tf_op jit(solution)/shard_map/pallas_call | solution.py:215
  44.8 0.2 collective-permute-start.3
  45.0 21.3 %all_to_all.11.terms_ref = bf16[16,256,128]{2,1,0:T(8,128)(2,1)S(1)} all-to-all(bf16[16,256,128]{2,1,0:T(8,128)(2,1)S(1)} %get-tuple-element.23), channel_id=1, replica_groups=mesh['x'=4,'yl'=2,'yh'=2,'c'=2,'z'=8] {'x','yl','yh'}, dimensions={0} | all-to-all | bytes 2097152 | tf_op jit(solution)/shard_map/all_to_all | solution.py:262
  66.3 0.0 collective-permute-done.3.recv_ref
  66.3 0.9 %shard_map.77 = (bf16[1024,128]{1,0:T(8,128)(2,1)}, bf16[1024,128]{1,0:T(8,128)(2,1)}, bf16[128,128]{1,0:T(8,128)(2,1)}, bf16[128,128]{1,0:T(8,128)(2,1)}) custom-call(f32[2048,128]{1,0:T(8,128)S(1)} %get-tuple-element.21.keep_ref, f32[2048,128]{1,0:T(8,128)S(1)} %collective-permute-done.3.recv_ref, bf16[16,256,128]{2,1,0:T(8,128)(2,1)S(1)} %all_to_all.11.terms_ref), custom_call_target="tpu_custom_call" | custom-call | tf_op jit(solution)/shard_map/pallas_call | solution.py:248
Async XLA Ops:
  0.6 1.8 %collective-permute-start = (bf16[1024,128]{1,0:T(8,128)(2,1)}, bf16[1024,128]{1,0:T(8,128)(2,1)S(1)}, u32[]{:S(2)}, u32[]{:S(2)}) collective-permute-start(bf16[1024,128]{1,0:T(8,128)(2,1)} %bitcast.8), channel_id=1, source_target_pairs={{0,8},{8,0},{1,9},{9,1},{2,10},{10,2},{3,11},{11,3},{4,12},{12,4},... | collective-permute-start | bytes 786440 | tf_op jit(solution)/shard_map/ppermute | solution.py:258
  0.7 2.1 %collective-permute-start.1 = (bf16[1024,128]{1,0:T(8,128)(2,1)}, bf16[1024,128]{1,0:T(8,128)(2,1)S(1)}, u32[]{:S(2)}, u32[]{:S(2)}) collective-permute-start(bf16[1024,128]{1,0:T(8,128)(2,1)} %bitcast.11), channel_id=1, source_target_pairs={{0,8},{8,0},{1,9},{9,1},{2,10},{10,2},{3,11},{11,3},{4,12},{12,4},... | collective-permute-start | bytes 786440 | tf_op jit(solution)/shard_map/ppermute | solution.py:258
  3.0 24.3 %copy-start = (bf16[128,8,128]{2,1,0:T(8,128)(2,1)S(1)}, bf16[128,8,128]{2,1,0:T(8,128)(2,1)}, u32[]{:S(2)}) copy-start(bf16[128,8,128]{2,1,0:T(8,128)(2,1)} %param.4) | copy-start | bytes 786436
  3.1 24.3 %copy-start.1 = (bf16[128,8,128]{2,1,0:T(8,128)(2,1)S(1)}, bf16[128,8,128]{2,1,0:T(8,128)(2,1)}, u32[]{:S(2)}) copy-start(bf16[128,8,128]{2,1,0:T(8,128)(2,1)} %param.7) | copy-start | bytes 786436
  33.1 1.5 %collective-permute-start.2 = (f32[8,2048]{1,0:T(8,128)S(1)}, f32[8,2048]{1,0:T(8,128)S(1)}, u32[]{:S(2)}, u32[]{:S(2)}) collective-permute-start(f32[8,2048]{1,0:T(8,128)S(1)} %get-tuple-element.19.stat_ref), channel_id=1, source_target_pairs={{0,8},{8,0},{1,9},{9,1},{2,10},{10,2},{3,11},{11,3},{4,12},{12,4},... | collective-permute-start | bytes 196616 | tf_op jit(solution)/shard_map/ppermute | solution.py:258
  44.8 21.5 %collective-permute-start.3 = (f32[2048,128]{1,0:T(8,128)S(1)}, f32[2048,128]{1,0:T(8,128)S(1)}, u32[]{:S(2)}, u32[]{:S(2)}) collective-permute-start(f32[2048,128]{1,0:T(8,128)S(1)} %get-tuple-element.22), channel_id=1, source_target_pairs={{0,8},{8,0},{1,9},{9,1},{2,10},{10,2},{3,11},{11,3},{4,12},{12,4},... | collective-permute-start | bytes 3145736 | tf_op jit(solution)/shard_map/ppermute | solution.py:258

commit v7 on v6

--- a/solution.py
+++ b/solution.py
@@ -36,7 +36,7 @@
     return slice(b * QB, (b + 1) * QB)
 
 
-def forward_kernel(q_ref, q2_ref, g_ref, g2_ref, kv_ref, stat_ref, half_ref, s0, s1):
+def forward_kernel(q_ref, q2_ref, g_ref, g2_ref, kv_ref, mark_ref, stat_ref, half_ref, s0, s1):
     own_rows = q_ref.shape[0]
     rows = 2 * own_rows
 
@@ -190,7 +190,7 @@
     )
 
 
-def forward(q, q2, g, g2, kv):
+def forward(q, q2, g, g2, kv, mark):
     n = q.shape[0]
     vmem = pl.BlockSpec(memory_space=pltpu.VMEM)
     return pl.pallas_call(
@@ -199,14 +199,14 @@
             jax.ShapeDtypeStruct((8, 2 * n), F32),
             jax.ShapeDtypeStruct((HEAD_DIM, 2 * n), F32),
         ),
-        in_specs=[vmem] * 5,
+        in_specs=[vmem] * 6,
         out_specs=(vmem,) * 2,
         scratch_shapes=[pltpu.VMEM((KEYS, QB), F32), pltpu.VMEM((KEYS, QB), F32)],
         cost_estimate=pl.CostEstimate(
             flops=8 * n * KEYS * HEAD_DIM, transcendentals=2 * n * KEYS, bytes_accessed=3 << 20
         ),
         compiler_params=pltpu.CompilerParams(vmem_limit_bytes=VMEM_LIMIT),
-    )(q, q2, g, g2, kv)
+    )(q, q2, g, g2, kv, mark)
 
 
 def backward(q, q2, g, g2, kv, stat, stat2, half):
@@ -265,11 +265,12 @@
 def step(queries, keys, values, out_grad):
     q = queries.reshape(-1, HEAD_DIM)
     g = out_grad.reshape(-1, HEAD_DIM)
-    q2, g2 = swap_cores(q), swap_cores(g)
+    q2 = swap_cores(q)
+    g2 = swap_cores(g)
     kv = jnp.concatenate([keys[:, 0, :], values[:, 0, :]], axis=0)
-    kv, q2, g2 = lax.optimization_barrier((jnp.broadcast_to(kv[None], (NCHIP,) + kv.shape), q2, g2))
-    kv = exchange(kv)
-    stat, half = forward(q, q2, g, g2, kv)
+    kv = exchange(jnp.broadcast_to(kv[None], (NCHIP,) + kv.shape))
+    mark = jnp.max(kv[:1, :16, :], axis=0)
+    stat, half = forward(q, q2, g, g2, kv, mark)
     keep, send, dkv = backward(q, q2, g, g2, kv, stat, swap_cores(stat), half)
     recv = swap_cores(send)
     terms = exchange(dkv)

time: 67.5 us -> 69 us (1.022)
  blocking collectives: 45.6 us -> 22.1 us
  waiting for transfers between devices: 2.07 us -> 18.8 us
  starting transfers between devices: 1.11 us -> 8.27 us
  local copies, waits for them, and re-layouts: 0.21 us -> 1.19 us
    all_to_all x2 -> x1, blocking collectives: 45.6 us -> 22.1 us  [exchange(): return lax.all_to_all(a, CHIPS, 0, 0, tiled=True)]
    all_to_all x0 -> x1, waiting for transfers between devices: none -> 17.6 us  [exchange(): return lax.all_to_all(a, CHIPS, 0, 0, tiled=True)]
    all_to_all x0 -> x1, starting transfers between devices: none -> 7.17 us  [exchange(): return lax.all_to_all(a, CHIPS, 0, 0, tiled=True)]
    broadcast_in_dim x1, local copies, waits for them, and re-layouts: 0.19 us -> 1.18 us  [step(): kv = exchange(jnp.broadcast_to(kv[None], (NCHIP,) + kv.shape))]
    ppermute x4, waiting for transfers between devices: 2.07 us -> 1.25 us  [swap_cores(): return lax.ppermute(a, 'c', [(0, 1), (1, 0)])]
  transfers between devices with their start and end apart: 4 -> 5, of which waited for: 3 -> 2; matrix products, arithmetic and copies ran while one was open for 1% -> 0% of each run, Pallas kernels for 0% -> 0%
where the time goes in v7:
time: 69 us; the launch traced here: 68.6 us
  blocking collectives  22.1 us (32%)
  waiting for transfers between devices  18.8 us (27%)
  Pallas kernels  16.8 us (24%)
  starting transfers between devices  8.27 us (12%)
  local copies, waits for them, and re-layouts  1.19 us (2%)
  other arithmetic  0.78 us (1%)
    all_to_all x1, blocking collectives, exchange(): return lax.all_to_all(a, CHIPS, 0, 0, tiled=True)  22.1 us
    all_to_all x1, waiting for transfers between devices, exchange(): return lax.all_to_all(a, CHIPS, 0, 0, tiled=True)  17.6 us
    pallas_call x1, Pallas kernels, backward(): pl.pallas_call(backward_kernel, out_shape=(jax.ShapeDtypeStruct((2 * n, H...  10.2 us
    all_to_all x1, starting transfers between devices, exchange(): return lax.all_to_all(a, CHIPS, 0, 0, tiled=True)  7.17 us
    pallas_call x1, Pallas kernels, forward(): pl.pallas_call(forward_kernel, out_shape=(jax.ShapeDtypeStruct((8, 2 * n)...  5.67 us
  transfers between devices with their start and end apart: 5, of which 2 were waited for; matrix products, arithmetic and copies ran while one was open for 0% of the time, Pallas kernels for 0%

profile of v7, /device:TPU:32, one launch (start us, length us, event | category | flops | bytes accessed | tf_op | source)
XLA Modules:
  0.0 68.6 jit_solution(14123627806838417358)
XLA Ops:
  0.6 0.8 %pad_maximum_fusion = bf16[256,128]{1,0:T(8,128)(2,1)S(1)} fusion(bf16[128,128]{1,0:T(8,128)(2,1)} %bitcast.16, bf16[128,128]{1,0:T(8,128)(2,1)} %bitcast.17), kind=kLoop, calls=%fused_computation | loop fusion | flops 131072 | bytes 131072 | tf_op jit(solution)/shard_map/concatenate | solution.py:270
  1.4 1.2 %broadcast_in_dim.2 = bf16[16,256,128]{2,1,0:T(8,128)(2,1)} broadcast(bf16[256,128]{1,0:T(8,128)(2,1)S(1)} %pad_maximum_fusion), dimensions={1,2} | broadcast | bytes 1114112 | tf_op jit(solution)/shard_map/broadcast_in_dim | solution.py:271
  2.6 0.0 copy-start
  2.6 0.0 copy-start.1
  2.6 7.2 %all-to-all-start = ((bf16[16,256,128]{2,1,0:T(8,128)(2,1)}), bf16[16,256,128]{2,1,0:T(8,128)(2,1)S(1)}, u32[]{:S(2)}, u32[]{:S(2)}) async-start(bf16[16,256,128]{2,1,0:T(8,128)(2,1)} %broadcast_in_dim.2), calls=%async_computation | async-start | bytes 2097152 | tf_op jit(solution)/shard_map/all_to_all | solution.py:262
  9.8 0.0 copy-done
  9.8 0.1 collective-permute-start
  9.9 0.0 copy-done.1
  9.9 0.5 collective-permute-start.1
  10.4 17.6 %all-to-all-done.kv_ref = bf16[16,256,128]{2,1,0:T(8,128)(2,1)S(1)} async-done(((bf16[16,256,128]{2,1,0:T(8,128)(2,1)}), bf16[16,256,128]{2,1,0:T(8,128)(2,1)S(1)}, u32[]{:S(2)}, u32[]{:S(2)}) %all-to-all-start) | async-done | bytes 1048608 | tf_op jit(solution)/shard_map/all_to_all | solution.py:262
  28.0 0.0 collective-permute-done.q2_ref
  28.0 0.0 collective-permute-done.1.g2_ref
  28.0 5.7 %shard_map.75 = (f32[8,2048]{1,0:T(8,128)S(1)}, f32[128,2048]{1,0:T(8,128)S(1)}) custom-call(bf16[1024,128]{1,0:T(8,128)(2,1)S(1)} %bitcast.11, bf16[1024,128]{1,0:T(8,128)(2,1)S(1)} %collective-permute-done.q2_ref, bf16[1024,128]{1,0:T(8,128)(2,1)S(1)} %bitcast.14, bf16[1024,128]{1,0:T(8,128)(2,1)S(1)} %collective-permute-done.1.g2_ref, ...), custom_call_target="tpu_custom_call" | custom-call | flops 2147483648 | bytes 3145728 | tf_op jit(solution)/shard_map/pallas_call | solution.py:196
  33.6 0.3 collective-permute-start.2
  33.9 1.2 %collective-permute-done.2.stat2_ref = f32[8,2048]{1,0:T(8,128)S(1)} collective-permute-done((f32[8,2048]{1,0:T(8,128)S(1)}, f32[8,2048]{1,0:T(8,128)S(1)}, u32[]{:S(2)}, u32[]{:S(2)}) %collective-permute-start.2) | collective-permute-done | bytes 65568 | tf_op jit(solution)/shard_map/ppermute | solution.py:258
  35.2 10.2 %shard_map.76 = (f32[2048,128]{1,0:T(8,128)S(1)}, f32[2048,128]{1,0:T(8,128)S(1)}, bf16[16,256,128]{2,1,0:T(8,128)(2,1)S(1)}) custom-call(bf16[1024,128]{1,0:T(8,128)(2,1)S(1)} %bitcast.12, bf16[1024,128]{1,0:T(8,128)(2,1)S(1)} %collective-permute-done.q2_ref, bf16[1024,128]{1,0:T(8,128)(2,1)S(1)} %bitcast.15, ...), custom_call_target="tpu_custom_call" | custom-call | flops 5368709120 | bytes 5242880 | tf_op jit(solution)/shard_map/pallas_call | solution.py:215
  45.4 0.2 collective-permute-start.3
  45.6 22.1 %all_to_all.10.terms_ref = bf16[16,256,128]{2,1,0:T(8,128)(2,1)S(1)} all-to-all(bf16[16,256,128]{2,1,0:T(8,128)(2,1)S(1)} %get-tuple-element.17), channel_id=1, replica_groups=mesh['x'=4,'yl'=2,'yh'=2,'c'=2,'z'=8] {'x','yl','yh'}, dimensions={0} | all-to-all | bytes 2097152 | tf_op jit(solution)/shard_map/all_to_all | solution.py:262
  67.7 0.0 collective-permute-done.3.recv_ref
  67.7 0.9 %shard_map.77 = (bf16[1024,128]{1,0:T(8,128)(2,1)}, bf16[1024,128]{1,0:T(8,128)(2,1)}, bf16[128,128]{1,0:T(8,128)(2,1)}, bf16[128,128]{1,0:T(8,128)(2,1)}) custom-call(f32[2048,128]{1,0:T(8,128)S(1)} %get-tuple-element.15.keep_ref, f32[2048,128]{1,0:T(8,128)S(1)} %collective-permute-done.3.recv_ref, bf16[16,256,128]{2,1,0:T(8,128)(2,1)S(1)} %all_to_all.10.terms_ref), custom_call_target="tpu_custom_call" | custom-call | tf_op jit(solution)/shard_map/pallas_call | solution.py:248
  (1 shorter events, 0.0 us)
Async XLA Ops:
  2.6 7.2 %copy-start = (bf16[128,8,128]{2,1,0:T(8,128)(2,1)S(1)}, bf16[128,8,128]{2,1,0:T(8,128)(2,1)}, u32[]{:S(2)}) copy-start(bf16[128,8,128]{2,1,0:T(8,128)(2,1)} %param.4) | copy-start | bytes 786436
  2.6 7.3 %copy-start.1 = (bf16[128,8,128]{2,1,0:T(8,128)(2,1)S(1)}, bf16[128,8,128]{2,1,0:T(8,128)(2,1)}, u32[]{:S(2)}) copy-start(bf16[128,8,128]{2,1,0:T(8,128)(2,1)} %param.7) | copy-start | bytes 786436
  2.6 25.4 %all-to-all-start = ((bf16[16,256,128]{2,1,0:T(8,128)(2,1)}), bf16[16,256,128]{2,1,0:T(8,128)(2,1)S(1)}, u32[]{:S(2)}, u32[]{:S(2)}) async-start(bf16[16,256,128]{2,1,0:T(8,128)(2,1)} %broadcast_in_dim.2), calls=%async_computation | async-start | bytes 2097152 | tf_op jit(solution)/shard_map/all_to_all | solution.py:262
  9.8 18.2 %collective-permute-start = (bf16[1024,128]{1,0:T(8,128)(2,1)S(1)}, bf16[1024,128]{1,0:T(8,128)(2,1)S(1)}, u32[]{:S(2)}, u32[]{:S(2)}) collective-permute-start(bf16[1024,128]{1,0:T(8,128)(2,1)S(1)} %bitcast.10), channel_id=1, source_target_pairs={{0,8},{8,0},{1,9},{9,1},{2,10},{10,2},{3,11},{11,3},{4,12},{12,4},... | collective-permute-start | bytes 786440 | tf_op jit(solution)/shard_map/ppermute | solution.py:258
  9.9 18.1 %collective-permute-start.1 = (bf16[1024,128]{1,0:T(8,128)(2,1)S(1)}, bf16[1024,128]{1,0:T(8,128)(2,1)S(1)}, u32[]{:S(2)}, u32[]{:S(2)}) collective-permute-start(bf16[1024,128]{1,0:T(8,128)(2,1)S(1)} %bitcast.13), channel_id=1, source_target_pairs={{0,8},{8,0},{1,9},{9,1},{2,10},{10,2},{3,11},{11,3},{4,12},{12,4},... | collective-permute-start | bytes 786440 | tf_op jit(solution)/shard_map/ppermute | solution.py:258
  33.6 1.5 %collective-permute-start.2 = (f32[8,2048]{1,0:T(8,128)S(1)}, f32[8,2048]{1,0:T(8,128)S(1)}, u32[]{:S(2)}, u32[]{:S(2)}) collective-permute-start(f32[8,2048]{1,0:T(8,128)S(1)} %get-tuple-element.13.stat_ref), channel_id=1, source_target_pairs={{0,8},{8,0},{1,9},{9,1},{2,10},{10,2},{3,11},{11,3},{4,12},{12,4},... | collective-permute-start | bytes 196616 | tf_op jit(solution)/shard_map/ppermute | solution.py:258
  45.4 22.3 %collective-permute-start.3 = (f32[2048,128]{1,0:T(8,128)S(1)}, f32[2048,128]{1,0:T(8,128)S(1)}, u32[]{:S(2)}, u32[]{:S(2)}) collective-permute-start(f32[2048,128]{1,0:T(8,128)S(1)} %get-tuple-element.16), channel_id=1, source_target_pairs={{0,8},{8,0},{1,9},{9,1},{2,10},{10,2},{3,11},{11,3},{4,12},{12,4},... | collective-permute-start | bytes 3145736 | tf_op jit(solution)/shard_map/ppermute | solution.py:258

commit v8 on v7

--- a/solution.py
+++ b/solution.py
@@ -18,7 +18,7 @@
 KEYS = NCHIP * ROWS
 QB = 256
 KF = 512
-KB = 512
+KB = 1024
 VMEM_LIMIT = 32 << 20
 F32 = jnp.float32
 BF16 = jnp.bfloat16
@@ -153,10 +153,10 @@
             )
 
         def value_grad(c, lo):
-            store(c, 1, lo, dot(p_bufs[c % 2][lo:lo + KB // 2, :], g_all[...]))
+            store(c, 1, lo, dot(p_bufs[c % 2][lo:lo + KB, :], g_all[...]))
 
         def key_grad(c, lo):
-            store(c, 0, lo, dot(ds_bufs[c % 2][lo:lo + KB // 2, :], q_all[...]) * SCALE)
+            store(c, 0, lo, dot(ds_bufs[c % 2][lo:lo + KB, :], q_all[...]) * SCALE)
 
         def query_grad(c, b):
             dqt[:, span(b)] += dot(kt[:, c * KB:(c + 1) * KB], ds_bufs[c % 2][:, span(b)])
@@ -167,11 +167,10 @@
                 if c < chunks:
                     score_grad(c, b)
                 if prior >= 0:
-                    if b < 2:
-                        value_grad(prior, b * (KB // 2))
-                    elif b < 4:
-                        key_grad(prior, (b - 2) * (KB // 2))
-                    else:
+                    if b == 0:
+                        value_grad(prior, 0)
+                        key_grad(prior, 0)
+                    elif b >= 4:
                         query_grad(prior, 2 * b - 8)
                         query_grad(prior, 2 * b - 7)
         for b in range(nq):

time: 69 us -> 68.8 us (level)
  no operation moved by 1% of the time
where the time goes in v8:
time: 68.8 us; the launch traced here: 68.5 us
  blocking collectives  22.1 us (32%)
  waiting for transfers between devices  18.8 us (27%)
  Pallas kernels  16.7 us (24%)
  starting transfers between devices  8.26 us (12%)
  local copies, waits for them, and re-layouts  1.19 us (2%)
  other arithmetic  0.78 us (1%)
  between operations  0.69 us (1%)
    all_to_all x1, blocking collectives, exchange(): return lax.all_to_all(a, CHIPS, 0, 0, tiled=True)  22.1 us
    all_to_all x1, waiting for transfers between devices, exchange(): return lax.all_to_all(a, CHIPS, 0, 0, tiled=True)  17.6 us
    pallas_call x1, Pallas kernels, backward(): pl.pallas_call(backward_kernel, out_shape=(jax.ShapeDtypeStruct((2 * n, H...  10.1 us
    all_to_all x1, starting transfers between devices, exchange(): return lax.all_to_all(a, CHIPS, 0, 0, tiled=True)  7.17 us
    pallas_call x1, Pallas kernels, forward(): pl.pallas_call(forward_kernel, out_shape=(jax.ShapeDtypeStruct((8, 2 * n)...  5.67 us
  transfers between devices with their start and end apart: 5, of which 2 were waited for; matrix products, arithmetic and copies ran while one was open for 0% of the time, Pallas kernels for 0%

profile of v8, /device:TPU:32, one launch (start us, length us, event | category | flops | bytes accessed | tf_op | source)
XLA Modules:
  0.0 68.5 jit_solution(3070434368717035365)
XLA Ops:
  0.6 0.8 %pad_maximum_fusion = bf16[256,128]{1,0:T(8,128)(2,1)S(1)} fusion(bf16[128,128]{1,0:T(8,128)(2,1)} %bitcast.16, bf16[128,128]{1,0:T(8,128)(2,1)} %bitcast.17), kind=kLoop, calls=%fused_computation | loop fusion | flops 131072 | bytes 131072 | tf_op jit(solution)/shard_map/concatenate | solution.py:269
  1.4 1.2 %broadcast_in_dim.2 = bf16[16,256,128]{2,1,0:T(8,128)(2,1)} broadcast(bf16[256,128]{1,0:T(8,128)(2,1)S(1)} %pad_maximum_fusion), dimensions={1,2} | broadcast | bytes 1114112 | tf_op jit(solution)/shard_map/broadcast_in_dim | solution.py:270
  2.6 0.0 copy-start
  2.6 0.0 copy-start.1
  2.6 7.2 %all-to-all-start = ((bf16[16,256,128]{2,1,0:T(8,128)(2,1)}), bf16[16,256,128]{2,1,0:T(8,128)(2,1)S(1)}, u32[]{:S(2)}, u32[]{:S(2)}) async-start(bf16[16,256,128]{2,1,0:T(8,128)(2,1)} %broadcast_in_dim.2), calls=%async_computation | async-start | bytes 2097152 | tf_op jit(solution)/shard_map/all_to_all | solution.py:261
  9.8 0.0 copy-done
  9.8 0.1 collective-permute-start
  9.9 0.0 copy-done.1
  9.9 0.5 collective-permute-start.1
  10.4 17.6 %all-to-all-done.kv_ref = bf16[16,256,128]{2,1,0:T(8,128)(2,1)S(1)} async-done(((bf16[16,256,128]{2,1,0:T(8,128)(2,1)}), bf16[16,256,128]{2,1,0:T(8,128)(2,1)S(1)}, u32[]{:S(2)}, u32[]{:S(2)}) %all-to-all-start) | async-done | bytes 1048608 | tf_op jit(solution)/shard_map/all_to_all | solution.py:261
  28.0 0.0 collective-permute-done.q2_ref
  28.0 0.0 collective-permute-done.1.g2_ref
  28.0 5.7 %shard_map.75 = (f32[8,2048]{1,0:T(8,128)S(1)}, f32[128,2048]{1,0:T(8,128)S(1)}) custom-call(bf16[1024,128]{1,0:T(8,128)(2,1)S(1)} %bitcast.11, bf16[1024,128]{1,0:T(8,128)(2,1)S(1)} %collective-permute-done.q2_ref, bf16[1024,128]{1,0:T(8,128)(2,1)S(1)} %bitcast.14, bf16[1024,128]{1,0:T(8,128)(2,1)S(1)} %collective-permute-done.1.g2_ref, ...), custom_call_target="tpu_custom_call" | custom-call | flops 2147483648 | bytes 3145728 | tf_op jit(solution)/shard_map/pallas_call | solution.py:195
  33.6 0.3 collective-permute-start.2
  33.9 1.2 %collective-permute-done.2.stat2_ref = f32[8,2048]{1,0:T(8,128)S(1)} collective-permute-done((f32[8,2048]{1,0:T(8,128)S(1)}, f32[8,2048]{1,0:T(8,128)S(1)}, u32[]{:S(2)}, u32[]{:S(2)}) %collective-permute-start.2) | collective-permute-done | bytes 65568 | tf_op jit(solution)/shard_map/ppermute | solution.py:257
  35.2 10.1 %shard_map.76 = (f32[2048,128]{1,0:T(8,128)S(1)}, f32[2048,128]{1,0:T(8,128)S(1)}, bf16[16,256,128]{2,1,0:T(8,128)(2,1)S(1)}) custom-call(bf16[1024,128]{1,0:T(8,128)(2,1)S(1)} %bitcast.12, bf16[1024,128]{1,0:T(8,128)(2,1)S(1)} %collective-permute-done.q2_ref, bf16[1024,128]{1,0:T(8,128)(2,1)S(1)} %bitcast.15, ...), custom_call_target="tpu_custom_call" | custom-call | flops 5368709120 | bytes 5242880 | tf_op jit(solution)/shard_map/pallas_call | solution.py:214
  45.3 0.2 collective-permute-start.3
  45.5 22.1 %all_to_all.10.terms_ref = bf16[16,256,128]{2,1,0:T(8,128)(2,1)S(1)} all-to-all(bf16[16,256,128]{2,1,0:T(8,128)(2,1)S(1)} %get-tuple-element.17), channel_id=1, replica_groups=mesh['x'=4,'yl'=2,'yh'=2,'c'=2,'z'=8] {'x','yl','yh'}, dimensions={0} | all-to-all | bytes 2097152 | tf_op jit(solution)/shard_map/all_to_all | solution.py:261
  67.6 0.0 collective-permute-done.3.recv_ref
  67.6 0.9 %shard_map.77 = (bf16[1024,128]{1,0:T(8,128)(2,1)}, bf16[1024,128]{1,0:T(8,128)(2,1)}, bf16[128,128]{1,0:T(8,128)(2,1)}, bf16[128,128]{1,0:T(8,128)(2,1)}) custom-call(f32[2048,128]{1,0:T(8,128)S(1)} %get-tuple-element.15.keep_ref, f32[2048,128]{1,0:T(8,128)S(1)} %collective-permute-done.3.recv_ref, bf16[16,256,128]{2,1,0:T(8,128)(2,1)S(1)} %all_to_all.10.terms_ref), custom_call_target="tpu_custom_call" | custom-call | tf_op jit(solution)/shard_map/pallas_call | solution.py:247
  (1 shorter events, 0.0 us)
Async XLA Ops:
  2.6 7.2 %copy-start = (bf16[128,8,128]{2,1,0:T(8,128)(2,1)S(1)}, bf16[128,8,128]{2,1,0:T(8,128)(2,1)}, u32[]{:S(2)}) copy-start(bf16[128,8,128]{2,1,0:T(8,128)(2,1)} %param.4) | copy-start | bytes 786436
  2.6 7.3 %copy-start.1 = (bf16[128,8,128]{2,1,0:T(8,128)(2,1)S(1)}, bf16[128,8,128]{2,1,0:T(8,128)(2,1)}, u32[]{:S(2)}) copy-start(bf16[128,8,128]{2,1,0:T(8,128)(2,1)} %param.7) | copy-start | bytes 786436
  2.6 25.4 %all-to-all-start = ((bf16[16,256,128]{2,1,0:T(8,128)(2,1)}), bf16[16,256,128]{2,1,0:T(8,128)(2,1)S(1)}, u32[]{:S(2)}, u32[]{:S(2)}) async-start(bf16[16,256,128]{2,1,0:T(8,128)(2,1)} %broadcast_in_dim.2), calls=%async_computation | async-start | bytes 2097152 | tf_op jit(solution)/shard_map/all_to_all | solution.py:261
  9.8 18.2 %collective-permute-start = (bf16[1024,128]{1,0:T(8,128)(2,1)S(1)}, bf16[1024,128]{1,0:T(8,128)(2,1)S(1)}, u32[]{:S(2)}, u32[]{:S(2)}) collective-permute-start(bf16[1024,128]{1,0:T(8,128)(2,1)S(1)} %bitcast.10), channel_id=1, source_target_pairs={{0,8},{8,0},{1,9},{9,1},{2,10},{10,2},{3,11},{11,3},{4,12},{12,4},... | collective-permute-start | bytes 786440 | tf_op jit(solution)/shard_map/ppermute | solution.py:257
  9.9 18.1 %collective-permute-start.1 = (bf16[1024,128]{1,0:T(8,128)(2,1)S(1)}, bf16[1024,128]{1,0:T(8,128)(2,1)S(1)}, u32[]{:S(2)}, u32[]{:S(2)}) collective-permute-start(bf16[1024,128]{1,0:T(8,128)(2,1)S(1)} %bitcast.13), channel_id=1, source_target_pairs={{0,8},{8,0},{1,9},{9,1},{2,10},{10,2},{3,11},{11,3},{4,12},{12,4},... | collective-permute-start | bytes 786440 | tf_op jit(solution)/shard_map/ppermute | solution.py:257
  33.6 1.5 %collective-permute-start.2 = (f32[8,2048]{1,0:T(8,128)S(1)}, f32[8,2048]{1,0:T(8,128)S(1)}, u32[]{:S(2)}, u32[]{:S(2)}) collective-permute-start(f32[8,2048]{1,0:T(8,128)S(1)} %get-tuple-element.13.stat_ref), channel_id=1, source_target_pairs={{0,8},{8,0},{1,9},{9,1},{2,10},{10,2},{3,11},{11,3},{4,12},{12,4},... | collective-permute-start | bytes 196616 | tf_op jit(solution)/shard_map/ppermute | solution.py:257
  45.3 22.3 %collective-permute-start.3 = (f32[2048,128]{1,0:T(8,128)S(1)}, f32[2048,128]{1,0:T(8,128)S(1)}, u32[]{:S(2)}, u32[]{:S(2)}) collective-permute-start(f32[2048,128]{1,0:T(8,128)S(1)} %get-tuple-element.16), channel_id=1, source_target_pairs={{0,8},{8,0},{1,9},{9,1},{2,10},{10,2},{3,11},{11,3},{4,12},{12,4},... | collective-permute-start | bytes 3145736 | tf_op jit(solution)/shard_map/ppermute | solution.py:257
